TPU v7x, 32 devices: a whole 2x2x4 slice. The times are simulated.
32 devices in a mesh: row: 16 (over z, x, core), col: 2 (over y).
Axes of the slice: x: 2, y: 2, z: 4, core: 2. Of those that a mesh axis runs over, the one named last changes fastest.
Arguments:
- ham: bfloat16 [8192, 8192], P('row'), may hold values from -0.2 to 1.7, as said below
- coeff: bfloat16 [8192, 8192], P('row', 'col'), may hold values from -40 to 40, as said below
- tile_mask: int32 [256, 256], P('row'), may hold values from 0 to 1, as said below
- occupation: int32 [16, 8192], replicated, may hold values from 0 to 1, as said below
- orbital_energy: float32 [16], replicated, may hold values from -0.4 to 0.6
- coulomb: float32 [16, 16], replicated, may hold values from 0.005 to 0.04
Outputs:
- correction: float32 [8192, 8192], P('row', 'col')
- stats: float32 [2], replicated
Inputs may be any that keep to these rules, and one draw needn't show every extreme that they name: ham is symmetric. coeff is symmetric. tile_mask is symmetric with ones on its diagonal. `occupation`: every column holds exactly 6 ones.
All inputs are finite; a program needn't handle non-finite values.
Results may differ from a plain program's by a relative error of at most 0.0003.
Values may be sent and summed in bfloat16 or wider, within the bound.
A program may use at most 192 MiB of HBM per device.

v0:
```python
import jax
import jax.numpy as jnp
from jax import lax
from jax.sharding import PartitionSpec as P

NS = 8192


def turn_tiles(product):
    tile_rows, tile_cols = product.shape
    row_count = lax.axis_size("row")
    col_count = lax.axis_size("col")
    fold_count = row_count // col_count
    sub_rows = tile_rows // col_count
    sectioned = product.reshape(col_count, sub_rows, tile_cols)
    sectioned = lax.all_to_all(sectioned, "col", split_axis=0, concat_axis=0, tiled=True)
    sectioned = sectioned.reshape(col_count, sub_rows, fold_count, tile_rows)
    sectioned = jnp.transpose(sectioned, (0, 2, 1, 3)).reshape(row_count, sub_rows, tile_rows)
    sectioned = lax.all_to_all(
        lax.all_to_all(sectioned, "row", split_axis=0, concat_axis=0, tiled=True),
        "col",
        split_axis=0,
        concat_axis=0,
        tiled=True,
    )
    sectioned = sectioned.reshape(col_count, fold_count, sub_rows, tile_rows)
    turned = jnp.transpose(sectioned, (3, 1, 0, 2)).reshape(tile_rows, tile_cols)
    return turned


def body(ham, coeff, tile_mask, occupation, orbital_energy, coulomb):
    tile_rows, strings = ham.shape
    tile_cols = coeff.shape[1]
    mask_cols = tile_mask.shape[1]
    block_size = strings // mask_cols
    mask_rows = tile_rows // block_size
    weights = tile_mask.astype(jnp.bfloat16)[:, None, :, None]
    masked = (ham.reshape(mask_rows, block_size, mask_cols, block_size) * weights).reshape(
        tile_rows, strings
    )
    occ_float = occupation.astype(jnp.float32)
    occ_alpha = lax.dynamic_slice_in_dim(occ_float, lax.axis_index("row") * tile_rows, tile_rows, 1)
    occ_beta = lax.dynamic_slice_in_dim(occ_float, lax.axis_index("col") * tile_cols, tile_cols, 1)
    energy_alpha = jnp.dot(orbital_energy, occ_alpha, precision=lax.Precision.HIGHEST)
    energy_beta = jnp.dot(orbital_energy, occ_beta, precision=lax.Precision.HIGHEST)
    coupling = jnp.dot(
        jnp.dot(occ_alpha.T, coulomb, precision=lax.Precision.HIGHEST),
        occ_beta,
        precision=lax.Precision.HIGHEST,
    )
    diagonal = energy_alpha[:, None] + energy_beta[None, :] + coupling
    product = jnp.dot(
        masked, lax.all_gather(coeff, "row", axis=0, tiled=True), preferred_element_type=jnp.float32
    )
    coeff_float = coeff.astype(jnp.float32)
    sigma = product + turn_tiles(product)
    late = lax.psum(
        (jnp.sum(coeff_float * sigma), jnp.sum(coeff_float * coeff_float)), ("row", "col")
    )
    projection = late[0]
    weight_sum = late[1]
    theta = projection / weight_sum
    residual = sigma - theta * coeff_float
    update = residual / jnp.maximum(jnp.abs(diagonal - theta), 1.0)
    totals = lax.psum((jnp.sum(residual * residual), jnp.sum(update * update)), ("row", "col"))
    correction = update * lax.rsqrt(totals[1] / (NS * NS) + 1e-06)
    stats = jnp.stack([theta, jnp.sqrt(totals[0] / (NS * NS))])
    return (correction, stats)


def solution(mesh):
    in_specs = (P("row", None), P("row", "col"), P("row", None), P(), P(), P())
    out_specs = (P("row", "col"), P())
    return jax.shard_map(body, mesh=mesh, in_specs=in_specs, out_specs=out_specs, check_vma=False)
```

profile of v0, /device:TPU:0, one launch (start us, length us, event | category | flops | bytes accessed | tf_op | source)
XLA Modules:
  0.0 950.2 jit_solution(6359552921560628057)
XLA Ops:
  7.2 0.0 copy-start
  7.2 0.0 all-gather.2.cloned.1.call-start
  7.2 0.7 all-gather.2.cloned.1.call-update
  7.9 0.7 convert_element_type.9
  8.6 12.2 %mul.41 = bf16[16,32,256,32]{3,2,1,0:T(8,128)(2,1)} broadcast(bf16[16,256]{1,0:T(8,128)(2,1)S(1)} %convert_element_type.9), dimensions={0,2} | broadcast | bytes 8396800 | tf_op jit(solution)/shard_map/mul | solution.py:38
  20.8 42.1 %mul.42 = bf16[512,8192]{1,0:T(8,128)(2,1)} reshape(bf16[16,32,256,32]{3,2,1,0:T(8,128)(2,1)} %mul.41) | data formatting | bytes 16777216 | tf_op jit(solution)/shard_map/mul | solution.py:38
  62.9 275.5 %all-gather.2.cloned.1.call-done = bf16[8192,4096]{1,0:T(8,128)(2,1)} async-done(((bf16[512,4096]{1,0:T(8,128)(2,1)}), bf16[8192,4096]{1,0:T(8,128)(2,1)}) %all-gather.2.cloned.1.call-update) | async-done | bytes 67108880 | tf_op jit(solution)/shard_map/all_gather | solution.py:53
  338.5 45.6 %fusion.3 = f32[512,4096]{1,0:T(8,128)} fusion(bf16[8192,4096]{1,0:T(8,128)(2,1)} %all-gather.2.cloned.1.call-done, bf16[512,8192]{1,0:T(8,128)(2,1)} %param.6, bf16[512,8192]{1,0:T(8,128)(2,1)} %mul.42), kind=kOutput, calls=%fused_computation.9 | convolution fusion | flops 34363932672 | bytes 92274688 | tf_op jit(solution)/shard_map/dot_general | solution.py:52
  384.1 8.9 copy.9
  393.0 104.0 %all_to_all.15 = f32[2,256,4096]{1,2,0:T(8,128)} all-to-all(f32[2,256,4096]{1,2,0:T(8,128)} %copy.9), channel_id=1, replica_groups=mesh['row'=16,'col'=2] {'col'}, dimensions={0} | all-to-all | bytes 16777216 | tf_op jit(solution)/shard_map/all_to_all | solution.py:16
  497.0 8.7 copy.10
  505.7 186.8 %all_to_all.16 = f32[16,256,512]{2,1,0:T(8,128)} all-to-all(f32[16,256,512]{2,1,0:T(8,128)} %bitcast.25), channel_id=1, replica_groups=mesh['row'=16,'col'=2] {'row'}, dimensions={0} | all-to-all | bytes 16777216 | tf_op jit(solution)/shard_map/all_to_all | solution.py:20
  692.5 0.0 copy-start.3
  692.5 0.0 copy-start.4
  692.5 7.1 all-to-all-start.2
  699.5 0.0 copy-done.3
  699.6 0.0 copy-done.4
  699.6 0.1 fusion.10
  699.8 0.3 fusion.6
  700.1 0.0 copy-done
  700.1 0.2 fusion.8
  700.3 93.0 %all-to-all-done.2 = f32[16,256,512]{2,1,0:T(8,128)} async-done(((f32[16,256,512]{2,1,0:T(8,128)}), f32[16,256,512]{2,1,0:T(8,128)}, u32[]{:S(2)}, u32[]{:S(2)}) %all-to-all-start.2) | async-done | bytes 8388640 | tf_op jit(solution)/shard_map/all_to_all | solution.py:19
  793.3 13.3 %copy.11 = f32[512,8,2,256]{3,2,1,0:T(2,128)} copy(f32[512,8,2,256]{0,3,1,2:T(8,128)} %bitcast.5) | data formatting | bytes 16777216 | tf_op jit(solution)/shard_map/transpose | solution.py:27
  806.6 11.5 %reshape.29 = f32[512,4096]{1,0:T(8,128)} reshape(f32[512,8,2,256]{3,2,1,0:T(2,128)} %copy.11) | data formatting | bytes 16777216 | tf_op jit(solution)/shard_map/reshape | solution.py:27
  818.0 12.5 %fusion.1 = (f32[]{:T(128)}, f32[]{:T(128)}, f32[512,4096]{1,0:T(8,128)}) fusion(bf16[512,4096]{1,0:T(8,128)(2,1)} %param.7, f32[512,4096]{1,0:T(8,128)} %fusion.3, f32[512,4096]{1,0:T(8,128)} %reshape.29), kind=kLoop, calls=%fused_computation.4 | loop fusion | flops 12582910 | bytes 29360136 | tf_op jit(solution)/shard_map/reduce_sum | solution.py:58
  830.5 39.8 %all-reduce.1 = (f32[]{:T(128)}, f32[]{:T(128)}) all-reduce(f32[]{:T(128)} %get-tuple-element.3, f32[]{:T(128)} %get-tuple-element.2), channel_id=1, replica_groups=mesh['row'=16,'col'=2] {'row','col'}, use_global_device_ids=true, to_apply=%region_1.0 | all-reduce | flops 2 | bytes 16 | tf_op jit(solution)/shard_map/psum | solution.py:57
  871.6 0.0 copy-start.1
  871.6 0.0 copy-start.2
  871.6 7.5 multiply_reduce_fusion
  879.1 0.0 copy-done.1
  879.1 0.7 copy-done.2
  879.9 13.1 %multiply_reduce_fusion.1 = (f32[]{:T(128)}, f32[512,4096]{1,0:T(8,128)}) fusion(f32[512,16]{0,1:T(8,128)S(1)} %fusion.8, f32[16,8192]{1,0:T(8,128)S(1)} %convert_element_type.11, s32[]{:T(128)S(6)} %select_n.7, f32[4096]{0:T(1024)S(1)} %bitcast.26, f32[512]{0:T(512)S(1)} %bitcast.27, f32[512,4096]{1,0:T(8,128)S(1)} %copy-done.2, ...), kind=kOutput, calls=%fused_computation.7 | convolution fusion | flops 425721856 | bytes 21284876 | tf_op jit(solution)/shard_map/dot_general | solution.py:46
  893.0 40.7 %all-reduce = (f32[]{:T(128)}, f32[]{:T(128)}) all-reduce(f32[]{:T(128)} %get-tuple-element.9, f32[]{:T(128)} %multiply_reduce_fusion), channel_id=1, replica_groups=mesh['row'=16,'col'=2] {'row','col'}, use_global_device_ids=true, to_apply=%region_5.0 | all-reduce | flops 2 | bytes 16 | tf_op jit(solution)/shard_map/psum | solution.py:65
  934.9 0.6 pad_maximum_fusion
  935.5 7.9 broadcast_multiply_fusion
  (1 shorter events, 0.0 us)
Async XLA Ops:
  7.2 692.9 %copy-start = (f32[16,16]{1,0:T(8,128)S(1)}, f32[16,16]{1,0:T(8,128)}, u32[]{:S(2)}) copy-start(f32[16,16]{1,0:T(8,128)} %param.11) | copy-start | bytes 3076
  7.2 331.3 %all-gather.2.cloned.1.call-start = ((), (), s32[]{:S(2)}) async-start(), calls=%async_computation.3 | async-start | bytes 71303168 | tf_op jit(solution)/shard_map/all_gather | solution.py:53
  692.5 7.1 copy-start.3
  692.5 7.1 copy-start.4
  692.5 100.8 %all-to-all-start.2 = ((f32[16,256,512]{2,1,0:T(8,128)}), f32[16,256,512]{2,1,0:T(8,128)}, u32[]{:S(2)}, u32[]{:S(2)}) async-start(f32[16,256,512]{2,1,0:T(8,128)} %all_to_all.16), calls=%async_computation.2 | async-start | bytes 16777216 | tf_op jit(solution)/shard_map/all_to_all | solution.py:19
  871.6 7.5 copy-start.1
  871.6 8.2 copy-start.2
Sparse Core Ops, SparseCore 0:
  9.6 328.8 all-gather.1
where the time goes:
time: 953 us; the launch traced here: 950 us
  blocking collectives  371 us (39%)
  waiting for transfers between devices  369 us (39%)
  local copies, waits for them, and re-layouts  97.4 us (10%)
  matrix products  59.4 us (6%)
  other arithmetic  29.2 us (3%)
  between operations  16.7 us (2%)
    all_gather x1, waiting for transfers between devices, body(): lax.all_gather(coeff, 'row', axis=0, tiled=True)  276 us
    all_to_all x1, blocking collectives, turn_tiles(): lax.all_to_all(sectioned, 'row', split_axis=0, concat_axis=0, tiled=True)  187 us
    all_to_all x1, blocking collectives, turn_tiles(): lax.all_to_all(sectioned, 'col', split_axis=0, concat_axis=0, tiled=True)  104 us
    all_to_all x1, waiting for transfers between devices, turn_tiles(): lax.all_to_all(lax.all_to_all(sectioned, 'row', split_axis=0, concat_axis...  93 us
    mul x2, local copies, waits for them, and re-layouts, body(): ham.reshape(mask_rows, block_size, mask_cols, block_size) * weights  54.3 us
    dot_general x1, matrix products, body(): jnp.dot(masked, lax.all_gather(coeff, 'row', axis=0, tiled=True), preferr...  45.6 us
    psum x1, blocking collectives, body(): lax.psum((jnp.sum(residual * residual), jnp.sum(update * update)), ('row'...  40.7 us
    psum x1, blocking collectives, body(): lax.psum((jnp.sum(coeff_float * sigma), jnp.sum(coeff_float * coeff_float...  39.8 us
  transfers between devices with their start and end apart: 2, of which 2 were waited for; matrix products, arithmetic and copies ran while one was open for 6% of the time, Pallas kernels for 0%

commit v1 on v0

v1 whole, which is shorter than its diff:
```python
import functools

import jax
import jax.numpy as jnp
from jax import lax
from jax.experimental import pallas as pl
from jax.experimental.pallas import tpu as pltpu
from jax.sharding import PartitionSpec as P

MESH = pl.DeviceIdType.MESH
HIGH = lax.Precision.HIGHEST


def turn_kernel(
    row_count,
    col_count,
    total,
    p_ref,
    c_ref,
    left_ref,
    right_ref,
    out_ref,
    stats_ref,
    recv,
    relay_a,
    relay_b,
    mine,
    sums,
    own_send,
    recv_sem,
    arrive_a,
    arrive_b,
    relay_send,
    sum_send,
    sum_recv,
):
    row = lax.axis_index("row")
    col = lax.axis_index("col")
    tile = p_ref.shape[0]
    half = tile // 2
    fold = row_count // col_count
    home = lax.div(row, fold)
    place = lax.rem(row, fold)
    count = row_count * col_count
    me = row * col_count + col
    is_home = home == col

    barrier = pltpu.get_barrier_semaphore()

    def greet(d, carry):
        other = lax.rem(me + d, count)
        pl.semaphore_signal(
            barrier,
            inc=1,
            device_id=(lax.div(other, col_count), lax.rem(other, col_count)),
            device_id_type=MESH,
        )
        return carry

    lax.fori_loop(1, count, greet, 0)
    pl.semaphore_wait(barrier, count - 1)

    def columns(s):
        return pl.ds(pl.multiple_of(s * tile, tile), tile)

    def remote(src, dst, send, arrive, to_row, to_col):
        return pltpu.make_async_remote_copy(
            src_ref=src,
            dst_ref=dst,
            send_sem=send,
            recv_sem=arrive,
            device_id=(to_row, to_col),
            device_id_type=MESH,
        )

    def own_copies(k):
        s = lax.rem(place + k, fold)
        upper = p_ref.at[pl.ds(0, half), columns(s)]
        lower = p_ref.at[pl.ds(half, half), columns(s)]
        near = col * fold + s
        slot_a = col - (col > home).astype(jnp.int32)
        slot_b = row - fold * (home > col).astype(jnp.int32)
        direct = (
            remote(upper, recv.at[place, pl.ds(0, half)], own_send.at[k, 0], recv_sem.at[place, 0], near, col),
            remote(lower, recv.at[place, pl.ds(half, half)], own_send.at[k, 1], recv_sem.at[place, 1], near, col),
        )
        return direct, upper, lower, s, near, slot_a, slot_b

    def own_relayed(k):
        _, upper, lower, s, near, slot_a, slot_b = own_copies(k)
        return (
            remote(upper, relay_a.at[slot_a, s], own_send.at[k, 0], arrive_a.at[slot_a, s], row, home),
            remote(lower, relay_b.at[slot_b], own_send.at[k, 1], arrive_b.at[slot_b], near, col),
        )

    def exchange(phase, start):
        def one(d, carry):
            other = lax.rem(me + d, count)
            copy = remote(
                mine.at[phase],
                sums.at[phase, me],
                sum_send.at[phase, d],
                sum_recv.at[phase, me],
                lax.div(other, col_count),
                lax.rem(other, col_count),
            )
            if start:
                copy.start()
            else:
                copy.wait_send()
            return carry

        lax.fori_loop(1, count, one, 0)

    def gather_sums(phase):
        def one(d, carry):
            other = lax.rem(me + d, count)
            remote(
                mine.at[phase],
                sums.at[phase, other],
                sum_send.at[phase, d],
                sum_recv.at[phase, other],
                lax.div(other, col_count),
                lax.rem(other, col_count),
            ).wait_recv()
            return carry

        lax.fori_loop(1, count, one, 0)
        sums[phase, pl.ds(me, 1)] = mine[pl.ds(phase, 1)]
        every = jnp.sum(sums[phase], axis=0)
        return jnp.sum(every[0:8]), jnp.sum(every[8:16])

    def fold_sum(x):
        lanes = x.shape[1] // 128
        out = x[:, 0:128]
        for q in range(1, lanes):
            out = out + x[:, q * 128 : (q + 1) * 128]
        return jnp.sum(out.reshape(x.shape[0] // 8, 8, 128), axis=0)

    step_rows = min(32, tile)

    def early(r, carry):
        rows = pl.ds(pl.multiple_of(r * step_rows, step_rows), step_rows)
        c = c_ref[rows, :].astype(jnp.float32)
        return carry[0] + fold_sum(c * p_ref[rows, :]), carry[1] + fold_sum(c * c)

    zero = jnp.zeros((8, 128), jnp.float32)
    proj, weight = lax.fori_loop(0, tile // step_rows, early, (zero, zero))
    mine[0, 0:8] = proj
    mine[0, 8:16] = weight
    exchange(0, True)

    @pl.when(is_home)
    def _():
        def send(k, carry):
            for copy in own_copies(k)[0]:
                copy.start()
            return carry

        lax.fori_loop(1, fold, send, 0)
        pltpu.make_async_copy(
            p_ref.at[pl.ds(0, half), columns(place)], recv.at[place, pl.ds(0, half)], recv_sem.at[place, 0]
        ).start()
        pltpu.make_async_copy(
            p_ref.at[pl.ds(half, half), columns(place)], recv.at[place, pl.ds(half, half)], recv_sem.at[place, 1]
        ).start()

    @pl.when(jnp.logical_not(is_home))
    def _():
        def send(k, carry):
            for copy in own_relayed(k):
                copy.start()
            return carry

        lax.fori_loop(0, fold, send, 0)

    def relays(t):
        slot = lax.div(t, fold)
        k = lax.rem(t, fold)
        group = slot + (slot >= col).astype(jnp.int32)
        s = lax.rem(place + k, fold)
        far = lax.rem(place - k + fold, fold)
        slot_b = slot * fold + far
        copy_a = remote(
            relay_a.at[slot, s],
            recv.at[place, pl.ds(0, half)],
            relay_send.at[t, 0],
            recv_sem.at[place, 0],
            group * fold + s,
            col,
        )
        copy_b = remote(
            relay_b.at[slot_b],
            recv.at[far, pl.ds(half, half)],
            relay_send.at[t, 1],
            recv_sem.at[far, 1],
            row,
            group,
        )
        return slot, s, slot_b, copy_a, copy_b

    relay_steps = (col_count - 1) * fold

    @pl.when(is_home)
    def _():
        def step(t, carry):
            slot, s, slot_b, copy_a, copy_b = relays(t)
            pltpu.make_async_copy(relay_a.at[slot, s], relay_a.at[slot, s], arrive_a.at[slot, s]).wait()
            copy_a.start()
            pltpu.make_async_copy(relay_b.at[slot_b], relay_b.at[slot_b], arrive_b.at[slot_b]).wait()
            copy_b.start()
            return carry

        lax.fori_loop(0, relay_steps, step, 0)

    proj, weight = gather_sums(0)
    theta = 2.0 * proj / weight

    piece = min(128, tile)

    def finish(k, carry):
        s = lax.rem(place - k + fold, fold)
        upper = recv.at[s, pl.ds(0, half)]
        lower = recv.at[s, pl.ds(half, half)]
        pltpu.make_async_copy(upper, upper, recv_sem.at[s, 0]).wait()
        pltpu.make_async_copy(lower, lower, recv_sem.at[s, 1]).wait()
        cols = columns(s)

        def part(r, carry):
            squares, spread = carry
            rows = pl.ds(pl.multiple_of(r * piece, piece), piece)
            turned = recv[s, :, rows].T
            diagonal = jnp.dot(
                left_ref[rows, :], right_ref[:, cols], precision=HIGH, preferred_element_type=jnp.float32
            )
            sigma = p_ref[rows, cols] + turned
            residual = sigma - theta * c_ref[rows, cols].astype(jnp.float32)
            update = residual / jnp.maximum(jnp.abs(diagonal - theta), 1.0)
            out_ref[rows, cols] = update
            return squares + fold_sum(residual * residual), spread + fold_sum(update * update)

        return lax.fori_loop(0, tile // piece, part, carry)

    squares, spread = lax.fori_loop(0, fold, finish, (zero, zero))
    mine[1, 0:8] = squares
    mine[1, 8:16] = spread
    exchange(1, True)
    squares, spread = gather_sums(1)
    stats_ref[0] = theta
    stats_ref[1] = squares / total
    stats_ref[2] = spread / total

    exchange(0, False)
    exchange(1, False)

    @pl.when(is_home)
    def _():
        def done(k, carry):
            for copy in own_copies(k)[0]:
                copy.wait_send()
            return carry

        lax.fori_loop(1, fold, done, 0)

        def done_relay(t, carry):
            _, _, _, copy_a, copy_b = relays(t)
            copy_a.wait_send()
            copy_b.wait_send()
            return carry

        lax.fori_loop(0, relay_steps, done_relay, 0)

    @pl.when(jnp.logical_not(is_home))
    def _():
        def done(k, carry):
            for copy in own_relayed(k):
                copy.wait_send()
            return carry

        lax.fori_loop(0, fold, done, 0)


def turn_and_finish(product, coeff, left, right, strings):
    tile_rows, tile_cols = product.shape
    row_count = lax.axis_size("row")
    col_count = lax.axis_size("col")
    fold = row_count // col_count
    count = row_count * col_count
    half = tile_rows // 2
    others = max(col_count - 1, 1)
    vmem = pl.BlockSpec(memory_space=pltpu.VMEM)
    dma = pltpu.SemaphoreType.DMA
    return pl.pallas_call(
        functools.partial(turn_kernel, row_count, col_count, float(strings) * float(strings)),
        out_shape=(
            jax.ShapeDtypeStruct((tile_rows, tile_cols), jnp.float32),
            jax.ShapeDtypeStruct((3,), jnp.float32),
        ),
        in_specs=[vmem] * 4,
        out_specs=(vmem, pl.BlockSpec(memory_space=pltpu.SMEM)),
        scratch_shapes=[
            pltpu.VMEM((fold, tile_rows, tile_rows), jnp.float32),
            pltpu.VMEM((others, fold, half, tile_rows), jnp.float32),
            pltpu.VMEM((others * fold, half, tile_rows), jnp.float32),
            pltpu.VMEM((2, 16, 128), jnp.float32),
            pltpu.VMEM((2, count, 16, 128), jnp.float32),
            dma((fold, 2)),
            dma((fold, 2)),
            dma((others, fold)),
            dma((others * fold,)),
            dma((others * fold, 2)),
            dma((2, count)),
            dma((2, count)),
        ],
        compiler_params=pltpu.CompilerParams(
            collective_id=0, has_side_effects=True, vmem_limit_bytes=60 * 1024 * 1024
        ),
        name="turn_and_finish",
    )(product, coeff, left, right)


def body(ham, coeff, tile_mask, occupation, orbital_energy, coulomb):
    tile_rows, strings = ham.shape
    tile_cols = coeff.shape[1]
    mask_cols = tile_mask.shape[1]
    block_size = strings // mask_cols
    mask_rows = tile_rows // block_size
    weights = tile_mask.astype(jnp.bfloat16)[:, None, :, None]
    masked = (ham.reshape(mask_rows, block_size, mask_cols, block_size) * weights).reshape(
        tile_rows, strings
    )
    occ_float = occupation.astype(jnp.float32)
    occ_alpha = lax.dynamic_slice_in_dim(occ_float, lax.axis_index("row") * tile_rows, tile_rows, 1)
    occ_beta = lax.dynamic_slice_in_dim(occ_float, lax.axis_index("col") * tile_cols, tile_cols, 1)
    energy_alpha = jnp.dot(orbital_energy, occ_alpha, precision=HIGH)
    energy_beta = jnp.dot(orbital_energy, occ_beta, precision=HIGH)
    mixed = jnp.dot(occ_alpha.T, coulomb, precision=HIGH)
    orbitals = occupation.shape[0]
    depth = -(-(orbitals + 2) // 128) * 128
    left = jnp.concatenate(
        [mixed, energy_alpha[:, None], jnp.ones((tile_rows, 1)), jnp.zeros((tile_rows, depth - orbitals - 2))],
        axis=1,
    )
    right = jnp.concatenate(
        [occ_beta, jnp.ones((1, tile_cols)), energy_beta[None, :], jnp.zeros((depth - orbitals - 2, tile_cols))],
        axis=0,
    )
    product = jnp.dot(
        masked, lax.all_gather(coeff, "row", axis=0, tiled=True), preferred_element_type=jnp.float32
    )
    update, sums = turn_and_finish(product, coeff, left, right, strings)
    correction = update * lax.rsqrt(sums[2] + 1e-06)
    stats = jnp.stack([sums[0], jnp.sqrt(sums[1])])
    return (correction, stats)


def solution(mesh):
    in_specs = (P("row", None), P("row", "col"), P("row", None), P(), P(), P())
    out_specs = (P("row", "col"), P())
    return jax.shard_map(body, mesh=mesh, in_specs=in_specs, out_specs=out_specs, check_vma=False)
```

time: 953 us -> 682 us (0.72)
  blocking collectives: 371 us -> 0 us
  Pallas kernels: 0 us -> 278 us
  waiting for transfers between devices: 369 us -> 270 us
  local copies, waits for them, and re-layouts: 97.4 us -> 57.1 us
  other arithmetic: 29.2 us -> 13.3 us
  matrix products: 59.4 us -> 47.2 us
    all_to_all x2 -> x0, blocking collectives: 291 us -> none  [the longest x1 187 us: turn_tiles(): lax.all_to_all(sectioned, 'row', split_axis=0, concat_axis=0, tiled=True)]
    pallas_call x0 -> x1, Pallas kernels: none -> 278 us  [turn_and_finish(): pl.pallas_call(functools.partial(turn_kernel, row_count, col_count, float...]
    all_to_all x1 -> x0, waiting for transfers between devices: 93 us -> none  [turn_tiles(): lax.all_to_all(lax.all_to_all(sectioned, 'row', split_axis=0, concat_axis...]
    psum x2 -> x0, blocking collectives: 80.5 us -> none  [the longest x1 40.7 us: body(): lax.psum((jnp.sum(residual * residual), jnp.sum(update * update)), ('row'...]
    transpose x2 -> x0, local copies, waits for them, and re-layouts: 21.9 us -> none  [the longest x1 13.3 us: turn_tiles(): jnp.transpose(sectioned, (3, 1, 0, 2)).reshape(tile_rows, tile_cols)]
    reshape x2 -> x0, local copies, waits for them, and re-layouts: 20.4 us -> none  [the longest x1 11.5 us: turn_tiles(): jnp.transpose(sectioned, (3, 1, 0, 2)).reshape(tile_rows, tile_cols)]
    reduce_sum x2 -> x0, other arithmetic: 20 us -> none  [the longest x1 12.5 us: body(): jnp.sum(coeff_float * coeff_float)]
    dot_general x4 -> x3, matrix products: 13.7 us -> 1.48 us  [the longest x1 0.6 us: body(): mixed = jnp.dot(occ_alpha.T, coulomb, precision=HIGH)]
  transfers between devices with their start and end apart: 2 -> 1, of which waited for: 2 -> 1; matrix products, arithmetic and copies ran while one was open for 6% -> 9% of each run, Pallas kernels for 0% -> 0%
where the time goes in v1:
time: 682 us; the launch traced here: 681 us
  Pallas kernels  278 us (41%)
  waiting for transfers between devices  270 us (40%)
  local copies, waits for them, and re-layouts  57.1 us (8%)
  matrix products  47.2 us (7%)
  between operations  15.5 us (2%)
  other arithmetic  13.3 us (2%)
    pallas_call x1, Pallas kernels, turn_and_finish(): pl.pallas_call(functools.partial(turn_kernel, row_count, col_count, float...  278 us
    all_gather x1, waiting for transfers between devices, body(): lax.all_gather(coeff, 'row', axis=0, tiled=True)  269 us
    mul x2, local copies, waits for them, and re-layouts, body(): ham.reshape(mask_rows, block_size, mask_cols, block_size) * weights  55.4 us
    dot_general x1, matrix products, body(): jnp.dot(masked, lax.all_gather(coeff, 'row', axis=0, tiled=True), preferr...  45.7 us
  transfers between devices with their start and end apart: 1, of which 1 were waited for; matrix products, arithmetic and copies ran while one was open for 9% of the time, Pallas kernels for 0%

profile of v1, /device:TPU:0, one launch (start us, length us, event | category | flops | bytes accessed | tf_op | source)
XLA Modules:
  0.0 680.9 jit_solution(1649888940320266042)
XLA Ops:
  7.2 0.0 copy-start
  7.2 0.0 all-gather.2.cloned.1.call-start
  7.2 0.7 all-gather.2.cloned.1.call-update
  7.9 0.1 pad.3.clone
  8.0 0.1 pad.8.clone
  8.1 1.1 convert_element_type.7
  9.2 0.1 pad.9.clone
  9.2 0.7 convert_element_type.6
  10.0 13.5 %mul.23 = bf16[16,32,256,32]{3,2,1,0:T(8,128)(2,1)} broadcast(bf16[16,256]{1,0:T(8,128)(2,1)S(1)} %convert_element_type.6), dimensions={0,2} | broadcast | bytes 8396800 | tf_op jit(solution)/shard_map/mul | solution.py:329
  23.4 0.0 copy-start.2
  23.4 41.9 %mul.24 = bf16[512,8192]{1,0:T(8,128)(2,1)} reshape(bf16[16,32,256,32]{3,2,1,0:T(8,128)(2,1)} %mul.23) | data formatting | bytes 16777216 | tf_op jit(solution)/shard_map/mul | solution.py:329
  65.4 0.0 copy-done.2
  65.4 0.6 convolution_bitcast_fusion
  66.0 0.0 copy-done
  66.0 0.6 fusion.3
  66.6 0.9 maximum_maximum_fusion.1.left_ref
  67.5 0.3 fusion.5
  67.8 1.5 maximum_maximum_fusion.right_ref
  69.3 269.1 %all-gather.2.cloned.1.call-done = bf16[8192,4096]{1,0:T(8,128)(2,1)} async-done(((bf16[512,4096]{1,0:T(8,128)(2,1)}), bf16[8192,4096]{1,0:T(8,128)(2,1)}) %all-gather.2.cloned.1.call-update) | async-done | bytes 67108880 | tf_op jit(solution)/shard_map/all_gather | solution.py:349
  338.4 45.7 %fusion.p_ref = f32[512,4096]{1,0:T(8,128)} fusion(bf16[8192,4096]{1,0:T(8,128)(2,1)} %all-gather.2.cloned.1.call-done, bf16[512,8192]{1,0:T(8,128)(2,1)} %param.6, bf16[512,8192]{1,0:T(8,128)(2,1)} %mul.24), kind=kOutput, calls=%fused_computation | convolution fusion | flops 34363932672 | bytes 92274688 | tf_op jit(solution)/shard_map/dot_general | solution.py:348
  384.1 278.1 %turn_and_finish.1 = (f32[512,4096]{1,0:T(8,128)}, f32[3]{0:T(128)}) custom-call(f32[512,4096]{1,0:T(8,128)} %fusion.p_ref, bf16[512,4096]{1,0:T(8,128)(2,1)} %c_ref.1, f32[512,128]{1,0:T(8,128)} %maximum_maximum_fusion.1.left_ref, f32[128,4096]{1,0:T(8,128)} %maximum_maximum_fusion.right_ref), custom_call_target="tpu_custom_call" | custom-call | tf_op jit(solution)/shard_map/turn_and_finish/pallas_call | solution.py:293
  662.2 1.4 fusion.10
  665.0 1.2 pad_maximum_fusion
  666.2 0.0 copy-start.1
  666.2 7.9 %broadcast_multiply_fusion = f32[512,4096]{1,0:T(8,128)} fusion(f32[512,4096]{1,0:T(8,128)} %get-tuple-element.4, f32[]{:T(128)} %bitcast.5), kind=kLoop, calls=%fused_computation.2 | loop fusion | flops 2097152 | bytes 16777220 | tf_op jit(solution)/shard_map/mul | solution.py:352
  674.1 0.0 copy-done.1
  (2 shorter events, 0.0 us)
Async XLA Ops:
  7.2 58.8 %copy-start = (f32[16,16]{1,0:T(8,128)S(1)}, f32[16,16]{1,0:T(8,128)}, u32[]{:S(2)}) copy-start(f32[16,16]{1,0:T(8,128)} %param.11) | copy-start | bytes 3076
  7.2 331.3 %all-gather.2.cloned.1.call-start = ((), (), s32[]{:S(2)}) async-start(), calls=%async_computation | async-start | bytes 71303168 | tf_op jit(solution)/shard_map/all_gather | solution.py:349
  23.4 41.9 %copy-start.2 = (f32[16]{0:T(128)S(1)}, f32[16]{0:T(128)}, u32[]{:S(2)}) copy-start(f32[16]{0:T(128)} %param.10) | copy-start | bytes 196
  666.2 7.9 %copy-start.1 = (f32[16,16]{1,0:T(8,128)S(1)}, f32[16,16]{1,0:T(8,128)}, u32[]{:S(2)}) copy-start(f32[16,16]{1,0:T(8,128)} %param.11) | copy-start | bytes 3076
Sparse Core Ops, SparseCore 0:
  9.6 328.8 all-gather.1

commit v2 on v1

--- a/solution.py
+++ b/solution.py
@@ -15,25 +15,32 @@
     row_count,
     col_count,
     total,
-    p_ref,
-    c_ref,
-    left_ref,
-    right_ref,
-    out_ref,
-    stats_ref,
-    recv,
-    relay_a,
-    relay_b,
-    mine,
-    sums,
-    own_send,
-    recv_sem,
-    arrive_a,
-    arrive_b,
-    relay_send,
-    sum_send,
-    sum_recv,
+    *refs,
 ):
+    chunks = refs[:-21]
+    (
+        c_ref,
+        left_ref,
+        right_ref,
+        out_ref,
+        stats_ref,
+        p_ref,
+        packed,
+        recv,
+        relay_a,
+        relay_b,
+        mine,
+        sums,
+        load_sem,
+        own_send,
+        recv_sem,
+        arrive_a,
+        arrive_b,
+        relay_send,
+        sum_send,
+        sum_recv,
+        self_sem,
+    ) = refs[-21:]
     row = lax.axis_index("row")
     col = lax.axis_index("col")
     tile = p_ref.shape[0]
@@ -44,6 +51,13 @@
     count = row_count * col_count
     me = row * col_count + col
     is_home = home == col
+    width = p_ref.shape[1] // len(chunks)
+    loads = [
+        pltpu.make_async_copy(chunk, p_ref.at[:, pl.ds(q * width, width)], load_sem.at[q])
+        for q, chunk in enumerate(chunks)
+    ]
+    for load in loads:
+        load.start()
 
     barrier = pltpu.get_barrier_semaphore()
 
@@ -59,6 +73,8 @@
 
     lax.fori_loop(1, count, greet, 0)
     pl.semaphore_wait(barrier, count - 1)
+    for load in loads:
+        load.wait()
 
     def columns(s):
         return pl.ds(pl.multiple_of(s * tile, tile), tile)
@@ -73,25 +89,39 @@
             device_id_type=MESH,
         )
 
-    def own_copies(k):
+    def own_direct(k):
         s = lax.rem(place + k, fold)
-        upper = p_ref.at[pl.ds(0, half), columns(s)]
-        lower = p_ref.at[pl.ds(half, half), columns(s)]
+        near = col * fold + s
+        return [
+            remote(packed.at[s, h], recv.at[place, h], own_send.at[s, h], recv_sem.at[place, h], near, col)
+            for h in range(2)
+        ]
+
+    def own_relayed(k):
+        s = lax.rem(place + k, fold)
         near = col * fold + s
         slot_a = col - (col > home).astype(jnp.int32)
         slot_b = row - fold * (home > col).astype(jnp.int32)
-        direct = (
-            remote(upper, recv.at[place, pl.ds(0, half)], own_send.at[k, 0], recv_sem.at[place, 0], near, col),
-            remote(lower, recv.at[place, pl.ds(half, half)], own_send.at[k, 1], recv_sem.at[place, 1], near, col),
-        )
-        return direct, upper, lower, s, near, slot_a, slot_b
-
-    def own_relayed(k):
-        _, upper, lower, s, near, slot_a, slot_b = own_copies(k)
-        return (
-            remote(upper, relay_a.at[slot_a, s], own_send.at[k, 0], arrive_a.at[slot_a, s], row, home),
-            remote(lower, relay_b.at[slot_b], own_send.at[k, 1], arrive_b.at[slot_b], near, col),
-        )
+        return [
+            remote(packed.at[s, 0], relay_a.at[slot_a, s], own_send.at[s, 0], arrive_a.at[slot_a, s], row, home),
+            remote(packed.at[s, 1], relay_b.at[slot_b], own_send.at[s, 1], arrive_b.at[slot_b], near, col),
+        ]
+
+    def own_local():
+        return [pltpu.make_async_copy(packed.at[place, h], recv.at[place, h], self_sem.at[h]) for h in range(2)]
+
+    def pack(k):
+        s = lax.rem(place + k, fold)
+        cols = columns(s)
+        for h in range(2):
+            peak = jnp.max(jnp.abs(p_ref[pl.ds(h * half, half), cols]), axis=0, keepdims=True)
+            code = jnp.floor(jnp.log2(jnp.maximum(peak, 1e-30)) * 128.0) + 2.0
+            grow = jnp.exp2(code * (-1.0 / 128.0)) * 32767.0
+            packed[s, h, pl.ds(half, 16)] = jnp.broadcast_to(code, (16, tile)).astype(jnp.int32).astype(jnp.int16)
+            rows = min(64, half)
+            for r in range(0, half, rows):
+                value = p_ref[pl.ds(h * half + r, rows), cols] * grow
+                packed[s, h, pl.ds(r, rows)] = jnp.floor(value + 0.5).astype(jnp.int32).astype(jnp.int16)
 
     def exchange(phase, start):
         def one(d, carry):
@@ -150,29 +180,29 @@
     mine[0, 8:16] = weight
     exchange(0, True)
 
+    def launch(k, carry):
+        pack(k)
+
+        @pl.when(jnp.logical_not(is_home))
+        def _():
+            for copy in own_relayed(k):
+                copy.start()
+
+        @pl.when(jnp.logical_and(is_home, k > 0))
+        def _():
+            for copy in own_direct(k):
+                copy.start()
+
+        return carry
+
+    lax.fori_loop(0, fold, launch, 0)
+
     @pl.when(is_home)
     def _():
-        def send(k, carry):
-            for copy in own_copies(k)[0]:
-                copy.start()
-            return carry
-
-        lax.fori_loop(1, fold, send, 0)
-        pltpu.make_async_copy(
-            p_ref.at[pl.ds(0, half), columns(place)], recv.at[place, pl.ds(0, half)], recv_sem.at[place, 0]
-        ).start()
-        pltpu.make_async_copy(
-            p_ref.at[pl.ds(half, half), columns(place)], recv.at[place, pl.ds(half, half)], recv_sem.at[place, 1]
-        ).start()
-
-    @pl.when(jnp.logical_not(is_home))
-    def _():
-        def send(k, carry):
-            for copy in own_relayed(k):
-                copy.start()
-            return carry
-
-        lax.fori_loop(0, fold, send, 0)
+        for copy in own_local():
+            copy.start()
+        for copy in own_local():
+            copy.wait()
 
     def relays(t):
         slot = lax.div(t, fold)
@@ -183,7 +213,7 @@
         slot_b = slot * fold + far
         copy_a = remote(
             relay_a.at[slot, s],
-            recv.at[place, pl.ds(0, half)],
+            recv.at[place, 0],
             relay_send.at[t, 0],
             recv_sem.at[place, 0],
             group * fold + s,
@@ -191,7 +221,7 @@
         )
         copy_b = remote(
             relay_b.at[slot_b],
-            recv.at[far, pl.ds(half, half)],
+            recv.at[far, 1],
             relay_send.at[t, 1],
             recv_sem.at[far, 1],
             row,
@@ -220,24 +250,31 @@
 
     def finish(k, carry):
         s = lax.rem(place - k + fold, fold)
-        upper = recv.at[s, pl.ds(0, half)]
-        lower = recv.at[s, pl.ds(half, half)]
-        pltpu.make_async_copy(upper, upper, recv_sem.at[s, 0]).wait()
-        pltpu.make_async_copy(lower, lower, recv_sem.at[s, 1]).wait()
-        cols = columns(s)
+
+        @pl.when(jnp.logical_not(jnp.logical_and(is_home, k == 0)))
+        def _():
+            for h in range(2):
+                pltpu.make_async_copy(recv.at[s, h], recv.at[s, h], recv_sem.at[s, h]).wait()
 
         def part(r, carry):
             squares, spread = carry
             rows = pl.ds(pl.multiple_of(r * piece, piece), piece)
-            turned = recv[s, :, rows].T
-            diagonal = jnp.dot(
-                left_ref[rows, :], right_ref[:, cols], precision=HIGH, preferred_element_type=jnp.float32
-            )
-            sigma = p_ref[rows, cols] + turned
-            residual = sigma - theta * c_ref[rows, cols].astype(jnp.float32)
-            update = residual / jnp.maximum(jnp.abs(diagonal - theta), 1.0)
-            out_ref[rows, cols] = update
-            return squares + fold_sum(residual * residual), spread + fold_sum(update * update)
+            for h in range(2):
+                cols = pl.ds(pl.multiple_of(s * tile + h * half, half), half)
+                code = recv[s, h, pl.ds(half, 16), rows].astype(jnp.int32).astype(jnp.float32)[0:1]
+                shrink = jnp.exp2(code * (1.0 / 128.0)) * (1.0 / 32767.0)
+                value = recv[s, h, pl.ds(0, half), rows].astype(jnp.int32).astype(jnp.float32)
+                turned = (value * shrink).T
+                diagonal = jnp.dot(
+                    left_ref[rows, :], right_ref[:, cols], precision=HIGH, preferred_element_type=jnp.float32
+                )
+                sigma = p_ref[rows, cols] + turned
+                residual = sigma - theta * c_ref[rows, cols].astype(jnp.float32)
+                update = residual / jnp.maximum(jnp.abs(diagonal - theta), 1.0)
+                out_ref[rows, cols] = update
+                squares = squares + fold_sum(residual * residual)
+                spread = spread + fold_sum(update * update)
+            return squares, spread
 
         return lax.fori_loop(0, tile // piece, part, carry)
 
@@ -256,7 +293,7 @@
     @pl.when(is_home)
     def _():
         def done(k, carry):
-            for copy in own_copies(k)[0]:
+            for copy in own_direct(k):
                 copy.wait_send()
             return carry
 
@@ -280,13 +317,13 @@
         lax.fori_loop(0, fold, done, 0)
 
 
-def turn_and_finish(product, coeff, left, right, strings):
-    tile_rows, tile_cols = product.shape
+def turn_and_finish(products, coeff, left, right, strings):
+    tile_rows, tile_cols = coeff.shape
     row_count = lax.axis_size("row")
     col_count = lax.axis_size("col")
     fold = row_count // col_count
     count = row_count * col_count
-    half = tile_rows // 2
+    tall = tile_rows // 2 + 16
     others = max(col_count - 1, 1)
     vmem = pl.BlockSpec(memory_space=pltpu.VMEM)
     dma = pltpu.SemaphoreType.DMA
@@ -296,14 +333,17 @@
             jax.ShapeDtypeStruct((tile_rows, tile_cols), jnp.float32),
             jax.ShapeDtypeStruct((3,), jnp.float32),
         ),
-        in_specs=[vmem] * 4,
+        in_specs=[pl.BlockSpec(memory_space=pl.ANY)] * len(products) + [vmem] * 3,
         out_specs=(vmem, pl.BlockSpec(memory_space=pltpu.SMEM)),
         scratch_shapes=[
-            pltpu.VMEM((fold, tile_rows, tile_rows), jnp.float32),
-            pltpu.VMEM((others, fold, half, tile_rows), jnp.float32),
-            pltpu.VMEM((others * fold, half, tile_rows), jnp.float32),
+            pltpu.VMEM((tile_rows, tile_cols), jnp.float32),
+            pltpu.VMEM((fold, 2, tall, tile_rows), jnp.int16),
+            pltpu.VMEM((fold, 2, tall, tile_rows), jnp.int16),
+            pltpu.VMEM((others, fold, tall, tile_rows), jnp.int16),
+            pltpu.VMEM((others * fold, tall, tile_rows), jnp.int16),
             pltpu.VMEM((2, 16, 128), jnp.float32),
             pltpu.VMEM((2, count, 16, 128), jnp.float32),
+            dma((len(products),)),
             dma((fold, 2)),
             dma((fold, 2)),
             dma((others, fold)),
@@ -311,12 +351,16 @@
             dma((others * fold, 2)),
             dma((2, count)),
             dma((2, count)),
+            dma((2,)),
         ],
         compiler_params=pltpu.CompilerParams(
             collective_id=0, has_side_effects=True, vmem_limit_bytes=60 * 1024 * 1024
         ),
         name="turn_and_finish",
-    )(product, coeff, left, right)
+    )(*products, coeff, left, right)
+
+
+CHUNKS = 2
 
 
 def body(ham, coeff, tile_mask, occupation, orbital_energy, coulomb):
@@ -345,10 +389,12 @@
         [occ_beta, jnp.ones((1, tile_cols)), energy_beta[None, :], jnp.zeros((depth - orbitals - 2, tile_cols))],
         axis=0,
     )
-    product = jnp.dot(
-        masked, lax.all_gather(coeff, "row", axis=0, tiled=True), preferred_element_type=jnp.float32
-    )
-    update, sums = turn_and_finish(product, coeff, left, right, strings)
+    width = tile_cols // CHUNKS
+    products = []
+    for q in range(CHUNKS):
+        gathered = lax.all_gather(coeff[:, q * width : (q + 1) * width], "row", axis=0, tiled=True)
+        products.append(jnp.dot(masked, gathered, preferred_element_type=jnp.float32))
+    update, sums = turn_and_finish(products, coeff, left, right, strings)
     correction = update * lax.rsqrt(sums[2] + 1e-06)
     stats = jnp.stack([sums[0], jnp.sqrt(sums[1])])
     return (correction, stats)

time: 682 us -> 563 us (0.83)
  Pallas kernels: 278 us -> 163 us
  waiting for transfers between devices: 270 us -> 255 us
  matrix products: 47.2 us -> 56 us
    pallas_call x1, Pallas kernels: 278 us -> 163 us  [turn_and_finish(): pl.pallas_call(functools.partial(turn_kernel, row_count, col_count, float...]
    all_gather x1 -> x2, waiting for transfers between devices: 269 us -> 254 us  [body(): lax.all_gather(coeff[:, q * width:(q + 1) * width], 'row', axis=0, tiled=...]
    dot_general x1 -> x2, matrix products: 45.7 us -> 54.5 us  [body(): jnp.dot(masked, gathered, preferred_element_type=jnp.float32)]
  transfers between devices with their start and end apart: 1 -> 2, of which waited for: 1 -> 2; matrix products, arithmetic and copies ran while one was open for 9% -> 15% of each run, Pallas kernels for 0% -> 0%
where the time goes in v2:
time: 563 us; the launch traced here: 562 us
  waiting for transfers between devices  255 us (45%)
  Pallas kernels  163 us (29%)
  local copies, waits for them, and re-layouts  60.8 us (11%)
  matrix products  56 us (10%)
  between operations  15.4 us (3%)
  other arithmetic  11.5 us (2%)
    all_gather x2, waiting for transfers between devices, body(): lax.all_gather(coeff[:, q * width:(q + 1) * width], 'row', axis=0, tiled=...  254 us
    pallas_call x1, Pallas kernels, turn_and_finish(): pl.pallas_call(functools.partial(turn_kernel, row_count, col_count, float...  163 us
    dot_general x2, matrix products, body(): jnp.dot(masked, gathered, preferred_element_type=jnp.float32)  54.5 us
    mul x2, local copies, waits for them, and re-layouts, body(): ham.reshape(mask_rows, block_size, mask_cols, block_size) * weights  54.3 us
  transfers between devices with their start and end apart: 2, of which 2 were waited for; matrix products, arithmetic and copies ran while one was open for 15% of the time, Pallas kernels for 0%

profile of v2, /device:TPU:0, one launch (start us, length us, event | category | flops | bytes accessed | tf_op | source)
XLA Modules:
  0.0 561.6 jit_solution(11816143247440763240)
XLA Ops:
  7.2 0.0 copy-start
  7.2 0.0 copy-start.2
  7.2 0.0 copy-start.3
  7.2 0.0 all-gather.5.cloned.1.call-start
  7.2 4.8 fusion.12
  12.0 0.0 all-gather.5.cloned.1.call-update
  12.1 0.0 all-gather.3.cloned.1.call-start
  12.1 0.7 all-gather.3.cloned.1.call-update
  12.8 0.1 pad.3.clone
  12.9 0.1 pad.8.clone
  13.0 0.0 copy-done.2
  13.0 0.1 pad.9.clone
  13.1 0.0 copy-done.3
  13.1 12.3 %mul.23 = bf16[16,32,256,32]{3,2,1,0:T(8,128)(2,1)} broadcast(bf16[16,256]{1,0:T(8,128)(2,1)S(1)} %convert_element_type.6), dimensions={0,2} | broadcast | bytes 8396800 | tf_op jit(solution)/shard_map/mul | solution.py:373
  25.4 0.0 copy-start.4
  25.4 42.1 %mul.24 = bf16[512,8192]{1,0:T(8,128)(2,1)} reshape(bf16[16,32,256,32]{3,2,1,0:T(8,128)(2,1)} %mul.23) | data formatting | bytes 16777216 | tf_op jit(solution)/shard_map/mul | solution.py:373
  67.5 0.0 copy-done.4
  67.5 0.6 convolution_bitcast_fusion
  68.1 0.0 copy-done
  68.1 0.6 fusion.5
  68.7 0.8 maximum_maximum_fusion.1.refs_3_
  69.6 0.3 fusion.7
  69.8 1.5 maximum_maximum_fusion.refs_4_
  71.4 111.6 %all-gather.5.cloned.1.call-done = bf16[8192,2048]{1,0:T(8,128)(2,1)} async-done(((bf16[512,2048]{1,0:T(8,128)(2,1)}), bf16[8192,2048]{1,0:T(8,128)(2,1)}) %all-gather.5.cloned.1.call-update) | async-done | bytes 33554448 | tf_op jit(solution)/shard_map/all_gather | solution.py:395
  183.0 27.2 %fusion.refs_1_ = f32[512,2048]{1,0:T(8,128)} fusion(bf16[8192,2048]{1,0:T(8,128)(2,1)} %all-gather.5.cloned.1.call-done, bf16[512,8192]{1,0:T(8,128)(2,1)} %param.6, bf16[512,8192]{1,0:T(8,128)(2,1)} %mul.24), kind=kOutput, calls=%fused_computation.1 | convolution fusion | flops 17184063488 | bytes 54525952 | tf_op jit(solution)/shard_map/dot_general | solution.py:396
  210.2 142.5 %all-gather.3.cloned.1.call-done = bf16[8192,2048]{1,0:T(8,128)(2,1)} async-done(((bf16[512,2048]{1,0:T(8,128)(2,1)}), bf16[8192,2048]{1,0:T(8,128)(2,1)}) %all-gather.3.cloned.1.call-update) | async-done | bytes 33554448 | tf_op jit(solution)/shard_map/all_gather | solution.py:395
  352.7 27.3 %fusion.2.refs_0_ = f32[512,2048]{1,0:T(8,128)} fusion(bf16[8192,2048]{1,0:T(8,128)(2,1)} %all-gather.3.cloned.1.call-done, bf16[512,8192]{1,0:T(8,128)(2,1)} %param.6, bf16[512,8192]{1,0:T(8,128)(2,1)} %mul.24), kind=kOutput, calls=%fused_computation.3 | convolution fusion | flops 17184063488 | bytes 54525952 | tf_op jit(solution)/shard_map/dot_general | solution.py:396
  380.0 163.1 %turn_and_finish.1 = (f32[512,4096]{1,0:T(8,128)}, f32[3]{0:T(128)}) custom-call(f32[512,2048]{1,0:T(8,128)} %fusion.2.refs_0_, f32[512,2048]{1,0:T(8,128)} %fusion.refs_1_, bf16[512,4096]{1,0:T(8,128)(2,1)} %refs_2_.1, f32[512,128]{1,0:T(8,128)} %maximum_maximum_fusion.1.refs_3_, f32[128,4096]{1,0:T(8,128)} %maximum_maximum_fusion.refs_4_), custom_call_target="tpu_custom_call" | custom-call | tf_op jit(solution)/shard_map/turn_and_finish/pallas_call | solution.py:330
  543.0 1.4 fusion.13
  545.7 1.2 pad_maximum_fusion
  546.9 0.0 copy-start.1
  546.9 7.9 %broadcast_multiply_fusion = f32[512,4096]{1,0:T(8,128)} fusion(f32[512,4096]{1,0:T(8,128)} %get-tuple-element.4, f32[]{:T(128)} %bitcast.5), kind=kLoop, calls=%fused_computation | loop fusion | flops 2097152 | bytes 16777220 | tf_op jit(solution)/shard_map/mul | solution.py:398
  554.8 0.0 copy-done.1
  (4 shorter events, 0.1 us)
Async XLA Ops:
  7.2 60.9 %copy-start = (f32[16,16]{1,0:T(8,128)S(1)}, f32[16,16]{1,0:T(8,128)}, u32[]{:S(2)}) copy-start(f32[16,16]{1,0:T(8,128)} %param.11) | copy-start | bytes 3076
  7.2 5.8 %copy-start.2 = (s32[16,8192]{1,0:T(8,128)S(1)}, s32[16,8192]{1,0:T(8,128)}, u32[]{:S(2)}) copy-start(s32[16,8192]{1,0:T(8,128)} %param.9) | copy-start | bytes 1572868
  7.2 5.9 %copy-start.3 = (s32[16,256]{1,0:T(8,128)S(1)}, s32[16,256]{1,0:T(8,128)}, u32[]{:S(2)}) copy-start(s32[16,256]{1,0:T(8,128)} %param.8) | copy-start | bytes 49156
  7.2 175.8 %all-gather.5.cloned.1.call-start = ((), (), s32[]{:S(2)}) async-start(), calls=%async_computation.1 | async-start | bytes 35651584 | tf_op jit(solution)/shard_map/all_gather | solution.py:395
  12.1 340.6 %all-gather.3.cloned.1.call-start = ((), (), s32[]{:S(2)}) async-start(), calls=%async_computation | async-start | bytes 35651584 | tf_op jit(solution)/shard_map/all_gather | solution.py:395
  25.4 42.1 %copy-start.4 = (f32[16]{0:T(128)S(1)}, f32[16]{0:T(128)}, u32[]{:S(2)}) copy-start(f32[16]{0:T(128)} %param.10) | copy-start | bytes 196
  546.9 7.9 %copy-start.1 = (f32[16,16]{1,0:T(8,128)S(1)}, f32[16,16]{1,0:T(8,128)}, u32[]{:S(2)}) copy-start(f32[16,16]{1,0:T(8,128)} %param.11) | copy-start | bytes 3076
Sparse Core Ops, SparseCore 0:
  12.2 170.7 all-gather.4
  184.6 168.0 all-gather.2

commit v3 on v2

v3 whole, which is shorter than its diff:
```python
import functools
import math

import jax
import jax.numpy as jnp
from jax import lax
from jax.experimental import pallas as pl
from jax.experimental.layout import Layout, with_layout_constraint
from jax.experimental.pallas import tpu as pltpu
from jax.sharding import PartitionSpec as P

MESH = pl.DeviceIdType.MESH
HIGH = lax.Precision.HIGHEST


def turn_kernel(row_count, col_count, total, chunk, chunks, *refs):
    last = chunk == chunks - 1
    if last:
        products, arrived = refs[:chunks], refs[chunks : 2 * chunks - 1]
        c_ref, left_ref, right_ref, out_ref, stats_ref, recv = refs[2 * chunks - 1 : 2 * chunks + 5]
        refs = refs[2 * chunks + 5 :]
        mine, sums, sum_send, sum_recv = refs[-4:]
    else:
        products = refs[:1]
        recv = refs[1]
        refs = refs[2:]
    p_ref, packed, relay_a, relay_b, load_sem, own_send, recv_sem, arrive_a, arrive_b, send_a, send_b, self_sem = refs[:12]
    row = lax.axis_index("row")
    col = lax.axis_index("col")
    tile = p_ref.shape[0]
    half = tile // 2
    fold = row_count // col_count
    per = fold // chunks
    home = lax.div(row, fold)
    place = lax.rem(row, fold)
    turn = lax.div(place, chunks)
    count = row_count * col_count
    me = row * col_count + col
    is_home = home == col
    takes = lax.rem(place, chunks) == chunk
    if last:
        loads = [
            pltpu.make_async_copy(
                product.at[:, pl.ds(k * tile, tile)],
                p_ref.at[:, pl.ds((q + chunks * k) * tile, tile)],
                load_sem.at[q * per + k],
            )
            for q, product in enumerate(products)
            for k in range(per)
        ]
    else:
        loads = [pltpu.make_async_copy(products[0], p_ref, load_sem.at[0])]
    for load in loads:
        load.start()

    barrier = pltpu.get_barrier_semaphore()

    def greet(d, carry):
        other = lax.rem(me + d, count)
        pl.semaphore_signal(
            barrier,
            inc=1,
            device_id=(lax.div(other, col_count), lax.rem(other, col_count)),
            device_id_type=MESH,
        )
        return carry

    lax.fori_loop(1, count, greet, 0)
    pl.semaphore_wait(barrier, count - 1)
    for load in loads:
        load.wait()

    def columns(s):
        return pl.ds(pl.multiple_of(s * tile, tile), tile)

    def remote(src, dst, send, arrive, to_row, to_col):
        return pltpu.make_async_remote_copy(
            src_ref=src,
            dst_ref=dst,
            send_sem=send,
            recv_sem=arrive,
            device_id=(to_row, to_col),
            device_id_type=MESH,
        )

    def spot(k):
        kk = lax.rem(turn + k, per)
        return kk, chunk + chunks * kk

    def own_direct(k):
        kk, s = spot(k)
        near = col * fold + s
        return [
            remote(packed.at[kk, h], recv.at[place, h], own_send.at[kk, h], recv_sem.at[place, h], near, col)
            for h in range(2)
        ]

    def own_relayed(k):
        kk, s = spot(k)
        near = col * fold + s
        slot_a = col - (col > home).astype(jnp.int32)
        slot_b = row - fold * (home > col).astype(jnp.int32)
        return [
            remote(packed.at[kk, 0], relay_a.at[slot_a, kk], own_send.at[kk, 0], arrive_a.at[slot_a, kk], row, home),
            remote(packed.at[kk, 1], relay_b.at[slot_b], own_send.at[kk, 1], arrive_b.at[slot_b], near, col),
        ]

    def own_local():
        return [pltpu.make_async_copy(packed.at[turn, h], recv.at[place, h], self_sem.at[h]) for h in range(2)]

    def pack(k):
        kk, s = spot(k)
        cols = columns(s) if last else columns(kk)
        for h in range(2):
            peak = jnp.max(jnp.abs(p_ref[pl.ds(h * half, half), cols]), axis=0, keepdims=True)
            code = jnp.floor(jnp.log2(jnp.maximum(peak, 1e-30)) * 128.0) + 2.0
            grow = jnp.exp2(code * (-1.0 / 128.0)) * 32767.0
            packed[kk, h, pl.ds(half, 16)] = jnp.broadcast_to(code, (16, tile)).astype(jnp.int32).astype(jnp.int16)
            rows = min(64, half)
            for r in range(0, half, rows):
                value = p_ref[pl.ds(h * half + r, rows), cols] * grow
                packed[kk, h, pl.ds(r, rows)] = jnp.floor(value + 0.5).astype(jnp.int32).astype(jnp.int16)

    def exchange(phase, start):
        def one(d, carry):
            other = lax.rem(me + d, count)
            copy = remote(
                mine.at[phase],
                sums.at[phase, me],
                sum_send.at[phase, d],
                sum_recv.at[phase, me],
                lax.div(other, col_count),
                lax.rem(other, col_count),
            )
            if start:
                copy.start()
            else:
                copy.wait_send()
            return carry

        lax.fori_loop(1, count, one, 0)

    def gather_sums(phase):
        def one(d, carry):
            other = lax.rem(me + d, count)
            remote(
                mine.at[phase],
                sums.at[phase, other],
                sum_send.at[phase, d],
                sum_recv.at[phase, other],
                lax.div(other, col_count),
                lax.rem(other, col_count),
            ).wait_recv()
            return carry

        lax.fori_loop(1, count, one, 0)
        sums[phase, pl.ds(me, 1)] = mine[pl.ds(phase, 1)]
        every = jnp.sum(sums[phase], axis=0)
        return jnp.sum(every[0:8]), jnp.sum(every[8:16])

    def fold_sum(x):
        lanes = x.shape[1] // 128
        out = x[:, 0:128]
        for q in range(1, lanes):
            out = out + x[:, q * 128 : (q + 1) * 128]
        return jnp.sum(out.reshape(x.shape[0] // 8, 8, 128), axis=0)

    zero = jnp.zeros((8, 128), jnp.float32)
    if last:
        step_rows = min(32, tile)

        def early(r, carry):
            rows = pl.ds(pl.multiple_of(r * step_rows, step_rows), step_rows)
            c = c_ref[rows, :].astype(jnp.float32)
            return carry[0] + fold_sum(c * p_ref[rows, :]), carry[1] + fold_sum(c * c)

        proj, weight = lax.fori_loop(0, tile // step_rows, early, (zero, zero))
        mine[0, 0:8] = proj
        mine[0, 8:16] = weight
        exchange(0, True)

    def launch(k, carry):
        pack(k)

        @pl.when(jnp.logical_not(is_home))
        def _():
            for copy in own_relayed(k):
                copy.start()

        @pl.when(jnp.logical_and(is_home, jnp.logical_or(k > 0, jnp.logical_not(takes))))
        def _():
            for copy in own_direct(k):
                copy.start()

        return carry

    lax.fori_loop(0, per, launch, 0)

    @pl.when(jnp.logical_and(is_home, takes))
    def _():
        for copy in own_local():
            copy.start()
        for copy in own_local():
            copy.wait()

    def relay_first(t):
        slot = lax.div(t, per)
        group = slot + (slot >= col).astype(jnp.int32)
        kk, s = spot(lax.rem(t, per))
        return slot, kk, remote(
            relay_a.at[slot, kk], recv.at[place, 0], send_a.at[t], recv_sem.at[place, 0], group * fold + s, col
        )

    def relay_second(t):
        slot = lax.div(t, fold)
        group = slot + (slot >= col).astype(jnp.int32)
        far = lax.rem(place - lax.rem(t, fold) + fold, fold)
        slot_b = slot * fold + far
        return slot_b, remote(
            relay_b.at[slot_b], recv.at[far, 1], send_b.at[t], recv_sem.at[far, 1], row, group
        )

    @pl.when(is_home)
    def _():
        def step(t, carry):
            slot, kk, copy = relay_first(t)
            pltpu.make_async_copy(relay_a.at[slot, kk], relay_a.at[slot, kk], arrive_a.at[slot, kk]).wait()
            copy.start()
            return carry

        lax.fori_loop(0, (col_count - 1) * per, step, 0)

    @pl.when(jnp.logical_and(is_home, takes))
    def _():
        def step(t, carry):
            slot_b, copy = relay_second(t)
            pltpu.make_async_copy(relay_b.at[slot_b], relay_b.at[slot_b], arrive_b.at[slot_b]).wait()
            copy.start()
            return carry

        lax.fori_loop(0, (col_count - 1) * fold, step, 0)

    def await_piece(k):
        s = lax.rem(place - k + fold, fold)

        @pl.when(jnp.logical_and(takes, jnp.logical_not(jnp.logical_and(is_home, k == 0))))
        def _():
            for h in range(2):
                pltpu.make_async_copy(recv.at[s, h], recv.at[s, h], recv_sem.at[s, h]).wait()

    def settle():
        @pl.when(is_home)
        def _():
            def done(k, carry):
                @pl.when(jnp.logical_or(k > 0, jnp.logical_not(takes)))
                def _():
                    for copy in own_direct(k):
                        copy.wait_send()

                return carry

            lax.fori_loop(0, per, done, 0)

            def done_first(t, carry):
                relay_first(t)[-1].wait_send()
                return carry

            lax.fori_loop(0, (col_count - 1) * per, done_first, 0)

        @pl.when(jnp.logical_and(is_home, takes))
        def _():
            def done_second(t, carry):
                relay_second(t)[-1].wait_send()
                return carry

            lax.fori_loop(0, (col_count - 1) * fold, done_second, 0)

        @pl.when(jnp.logical_not(is_home))
        def _():
            def done(k, carry):
                for copy in own_relayed(k):
                    copy.wait_send()
                return carry

            lax.fori_loop(0, per, done, 0)

    if not last:

        def hold(k, carry):
            await_piece(k)
            return carry

        lax.fori_loop(0, fold, hold, 0)
        settle()
        return

    for q, ready in enumerate(arrived):

        @pl.when(lax.rem(place, chunks) == q)
        def _():
            fetch = pltpu.make_async_copy(ready, recv, self_sem.at[2])
            fetch.start()
            fetch.wait()

    proj, weight = gather_sums(0)
    theta = 2.0 * proj / weight

    piece = min(128, tile)

    def finish(k, carry):
        s = lax.rem(place - k + fold, fold)

        await_piece(k)

        def part(r, carry):
            squares, spread = carry
            rows = pl.ds(pl.multiple_of(r * piece, piece), piece)
            for h in range(2):
                cols = pl.ds(pl.multiple_of(s * tile + h * half, half), half)
                code = recv[s, h, pl.ds(half, 16), rows].astype(jnp.int32).astype(jnp.float32)[0:1]
                shrink = jnp.exp2(code * (1.0 / 128.0)) * (1.0 / 32767.0)
                value = recv[s, h, pl.ds(0, half), rows].astype(jnp.int32).astype(jnp.float32)
                turned = (value * shrink).T
                diagonal = jnp.dot(
                    left_ref[rows, :], right_ref[:, cols], precision=HIGH, preferred_element_type=jnp.float32
                )
                sigma = p_ref[rows, cols] + turned
                residual = sigma - theta * c_ref[rows, cols].astype(jnp.float32)
                update = residual / jnp.maximum(jnp.abs(diagonal - theta), 1.0)
                out_ref[rows, cols] = update
                squares = squares + fold_sum(residual * residual)
                spread = spread + fold_sum(update * update)
            return squares, spread

        return lax.fori_loop(0, tile // piece, part, carry)

    squares, spread = lax.fori_loop(0, fold, finish, (zero, zero))
    mine[1, 0:8] = squares
    mine[1, 8:16] = spread
    exchange(1, True)
    squares, spread = gather_sums(1)
    stats_ref[0] = theta
    stats_ref[1] = squares / total
    stats_ref[2] = spread / total

    exchange(0, False)
    exchange(1, False)
    settle()


def turn(chunk, chunks, products, arrived, coeff, left, right, strings):
    tile_rows, tile_cols = coeff.shape
    row_count = lax.axis_size("row")
    col_count = lax.axis_size("col")
    fold = row_count // col_count
    per = fold // chunks
    count = row_count * col_count
    tall = tile_rows // 2 + 16
    others = max(col_count - 1, 1)
    vmem = pl.BlockSpec(memory_space=pltpu.VMEM)
    anywhere = pl.BlockSpec(memory_space=pl.ANY)
    dma = pltpu.SemaphoreType.DMA
    last = chunk == chunks - 1
    arrival = (fold, 2, tall, tile_rows)
    scratch = [
        pltpu.VMEM((tile_rows, tile_cols if last else tile_cols // chunks), jnp.float32),
        pltpu.VMEM((per, 2, tall, tile_rows), jnp.int16),
        pltpu.VMEM((others, per, tall, tile_rows), jnp.int16),
        pltpu.VMEM((others * fold, tall, tile_rows), jnp.int16),
        dma((fold,)),
        dma((per, 2)),
        dma((fold, 2)),
        dma((others, per)),
        dma((others * fold,)),
        dma((others * per,)),
        dma((others * fold,)),
        dma((3,)),
    ]
    if last:
        operands = (*products, *arrived, coeff, left, right)
        in_specs = [anywhere] * (2 * chunks - 1) + [vmem] * 3
        out_shape = (
            jax.ShapeDtypeStruct((tile_rows, tile_cols), jnp.float32),
            jax.ShapeDtypeStruct((3,), jnp.float32),
        )
        out_specs = (vmem, pl.BlockSpec(memory_space=pltpu.SMEM))
        scratch = [
            pltpu.VMEM(arrival, jnp.int16),
            *scratch,
            pltpu.VMEM((2, 16, 128), jnp.float32),
            pltpu.VMEM((2, count, 16, 128), jnp.float32),
            dma((2, count)),
            dma((2, count)),
        ]
    else:
        operands = (products[chunk],)
        in_specs = [anywhere]
        out_shape = jax.ShapeDtypeStruct(arrival, jnp.int16)
        out_specs = vmem
    return pl.pallas_call(
        functools.partial(turn_kernel, row_count, col_count, float(strings) * float(strings), chunk, chunks),
        out_shape=out_shape,
        in_specs=in_specs,
        out_specs=out_specs,
        scratch_shapes=scratch,
        compiler_params=pltpu.CompilerParams(
            collective_id=chunk, has_side_effects=True, vmem_limit_bytes=(60 if last else 24) * 1024 * 1024
        ),
        name=f"turn_{chunk}",
    )(*operands)


CHUNKS = 4


def body(ham, coeff, tile_mask, occupation, orbital_energy, coulomb):
    tile_rows, strings = ham.shape
    tile_cols = coeff.shape[1]
    mask_cols = tile_mask.shape[1]
    block_size = strings // mask_cols
    mask_rows = tile_rows // block_size
    weights = tile_mask.astype(jnp.bfloat16)[:, None, :, None]
    masked = (ham.reshape(mask_rows, block_size, mask_cols, block_size) * weights).reshape(
        tile_rows, strings
    )
    occ_float = occupation.astype(jnp.float32)
    occ_alpha = lax.dynamic_slice_in_dim(occ_float, lax.axis_index("row") * tile_rows, tile_rows, 1)
    occ_beta = lax.dynamic_slice_in_dim(occ_float, lax.axis_index("col") * tile_cols, tile_cols, 1)
    energy_alpha = jnp.dot(orbital_energy, occ_alpha, precision=HIGH)
    energy_beta = jnp.dot(orbital_energy, occ_beta, precision=HIGH)
    mixed = jnp.dot(occ_alpha.T, coulomb, precision=HIGH)
    orbitals = occupation.shape[0]
    depth = -(-(orbitals + 2) // 128) * 128
    left = jnp.concatenate(
        [mixed, energy_alpha[:, None], jnp.ones((tile_rows, 1)), jnp.zeros((tile_rows, depth - orbitals - 2))],
        axis=1,
    )
    right = jnp.concatenate(
        [occ_beta, jnp.ones((1, tile_cols)), energy_beta[None, :], jnp.zeros((depth - orbitals - 2, tile_cols))],
        axis=0,
    )
    fold = tile_cols // tile_rows
    chunks = math.gcd(CHUNKS, fold)
    products = []
    arrived = []
    for q in range(chunks):
        part = jnp.concatenate(
            [coeff[:, s * tile_rows : (s + 1) * tile_rows] for s in range(q, fold, chunks)], axis=1
        )
        gathered = with_layout_constraint(lax.all_gather(part, "row", axis=0, tiled=True), Layout((0, 1)))
        products.append(jnp.dot(masked, gathered, preferred_element_type=jnp.float32))
        result = turn(q, chunks, products, arrived, coeff, left, right, strings)
        if q < chunks - 1:
            arrived.append(result)
    update, sums = result
    correction = update * lax.rsqrt(sums[2] + 1e-06)
    stats = jnp.stack([sums[0], jnp.sqrt(sums[1])])
    return (correction, stats)


def solution(mesh):
    in_specs = (P("row", None), P("row", "col"), P("row", None), P(), P(), P())
    out_specs = (P("row", "col"), P())
    return jax.shard_map(body, mesh=mesh, in_specs=in_specs, out_specs=out_specs, check_vma=False)
```

time: 563 us -> 699 us (1.24)
  Pallas kernels: 163 us -> 244 us
  waiting for transfers between devices: 255 us -> 287 us
  other arithmetic: 11.5 us -> 25.6 us
    pallas_call x1 -> x4, Pallas kernels: 163 us -> 244 us  [turn(): pl.pallas_call(functools.partial(turn_kernel, row_count, col_count, float...]
    all_gather x2 -> x4, waiting for transfers between devices: 254 us -> 286 us  [body(): lax.all_gather(part, 'row', axis=0, tiled=True)]
    mul x0 -> x1, other arithmetic: none -> 9.58 us  [body(): ham.reshape(mask_rows, block_size, mask_cols, block_size) * weights]
    unnamed x10 -> x22, local copies, waits for them, and re-layouts: 0.03 us -> 7.49 us
    dot_general x2 -> x4, matrix products: 54.5 us -> 59.5 us  [body(): jnp.dot(masked, gathered, preferred_element_type=jnp.float32)]
  transfers between devices with their start and end apart: 2 -> 4, of which waited for: 2 -> 4; matrix products, arithmetic and copies ran while one was open for 15% -> 16% of each run, Pallas kernels for 0% -> 25%
where the time goes in v3:
time: 699 us; the launch traced here: 698 us
  waiting for transfers between devices  287 us (41%)
  Pallas kernels  244 us (35%)
  local copies, waits for them, and re-layouts  65.7 us (9%)
  matrix products  60.9 us (9%)
  other arithmetic  25.6 us (4%)
  between operations  15.3 us (2%)
    all_gather x4, waiting for transfers between devices, body(): lax.all_gather(part, 'row', axis=0, tiled=True)  286 us
    pallas_call x4, Pallas kernels, turn(): pl.pallas_call(functools.partial(turn_kernel, row_count, col_count, float...  244 us
    dot_general x4, matrix products, body(): jnp.dot(masked, gathered, preferred_element_type=jnp.float32)  59.5 us
    mul x2, local copies, waits for them, and re-layouts, body(): ham.reshape(mask_rows, block_size, mask_cols, block_size) * weights  54 us
  transfers between devices with their start and end apart: 4, of which 4 were waited for; matrix products, arithmetic and copies ran while one was open for 16% of the time, Pallas kernels for 25%

profile of v3, /device:TPU:0, one launch (start us, length us, event | category | flops | bytes accessed | tf_op | source)
XLA Modules:
  0.0 698.0 jit_solution(16999036322863069226)
XLA Ops:
  7.2 0.0 copy-start
  7.2 0.0 all-gather.5.cloned.1.call-start
  7.2 2.6 fusion.8
  9.8 0.0 copy-start.9
  9.9 1.1 pad_maximum_fusion
  11.0 0.0 all-gather.5.cloned.1.call-update
  11.0 0.0 all-gather.7.cloned.1.call-start
  11.1 1.1 pad_maximum_fusion.1
  12.2 0.0 all-gather.7.cloned.1.call-update
  12.2 0.0 all-gather.9.cloned.1.call-start
  12.3 1.1 pad_maximum_fusion.2
  13.4 0.0 all-gather.9.cloned.1.call-update
  13.4 0.0 all-gather.11.cloned.1.call-start
  13.5 1.2 pad_maximum_fusion.3
  14.6 0.0 all-gather.11.cloned.1.call-update
  14.7 0.1 pad.8.clone
  14.7 0.1 pad.3.clone
  14.8 0.0 copy-done.9
  14.8 12.0 %mul.23 = bf16[16,32,256,32]{3,2,1,0:T(8,128)(2,1)} broadcast(bf16[16,256]{1,0:T(8,128)(2,1)S(1)} %convert_element_type.6), dimensions={0,2} | broadcast | bytes 8396800 | tf_op jit(solution)/shard_map/mul | solution.py:423
  26.8 0.0 copy-start.8
  26.8 42.1 %mul.24 = bf16[512,8192]{1,0:T(8,128)(2,1)} reshape(bf16[16,32,256,32]{3,2,1,0:T(8,128)(2,1)} %mul.23) | data formatting | bytes 16777216 | tf_op jit(solution)/shard_map/mul | solution.py:423
  68.9 0.0 copy-done.8
  68.9 0.1 pad.9.clone
  69.0 0.0 copy-start.10
  69.0 9.6 %mul.25 = bf16[512,8192]{1,0:T(8,128)(2,1)} multiply(bf16[512,8192]{1,0:T(8,128)(2,1)} %param.6, bf16[512,8192]{1,0:T(8,128)(2,1)} %mul.24) | non-fusion elementwise | flops 4194304 | bytes 25165824 | tf_op jit(solution)/shard_map/mul | solution.py:423
  78.6 0.0 copy-done.10
  78.6 0.6 convolution_bitcast_fusion
  79.2 0.0 copy-done
  79.2 0.6 fusion.1
  79.8 0.8 maximum_maximum_fusion.1.refs_8_
  80.7 0.3 fusion.3
  80.9 1.6 maximum_maximum_fusion.refs_9_
  82.5 57.8 %all-gather.5.cloned.1.call-done = bf16[8192,1024]{1,0:T(8,128)(2,1)} async-done(((bf16[512,1024]{1,0:T(8,128)(2,1)}), bf16[8192,1024]{1,0:T(8,128)(2,1)}) %all-gather.5.cloned.1.call-update) | async-done | bytes 16777232 | tf_op jit(solution)/shard_map/all_gather | solution.py:450
  140.3 14.6 %fusion.10.refs_0_ = f32[512,1024]{1,0:T(8,128)S(1)} fusion(bf16[512,8192]{1,0:T(8,128)(2,1)} %mul.25, bf16[8192,1024]{1,0:T(8,128)(2,1)} %all-gather.5.cloned.1.call-done), kind=kOutput, calls=%fused_computation.20 | convolution fusion | flops 8589934592 | bytes 27262976 | tf_op jit(solution)/shard_map/dot_general | solution.py:451
  154.9 0.0 copy-start.5
  154.9 67.1 %turn_0.1.refs_4_ = s16[8,2,272,512]{3,2,1,0:T(8,128)(2,1)S(1)} custom-call(f32[512,1024]{1,0:T(8,128)S(1)} %fusion.10.refs_0_), custom_call_target="tpu_custom_call" | custom-call | tf_op jit(solution)/shard_map/turn_0/pallas_call | solution.py:400
  222.0 0.0 copy-start.2
  222.1 2.1 copy-done.2
  224.1 66.9 %all-gather.7.cloned.1.call-done = bf16[8192,1024]{1,0:T(8,128)(2,1)} async-done(((bf16[512,1024]{1,0:T(8,128)(2,1)}), bf16[8192,1024]{1,0:T(8,128)(2,1)}) %all-gather.7.cloned.1.call-update) | async-done | bytes 16777232 | tf_op jit(solution)/shard_map/all_gather | solution.py:450
  291.0 14.6 %fusion.11.refs_0_.refs_1_ = f32[512,1024]{1,0:T(8,128)S(1)} fusion(bf16[512,8192]{1,0:T(8,128)(2,1)} %mul.25, bf16[8192,1024]{1,0:T(8,128)(2,1)} %all-gather.7.cloned.1.call-done), kind=kOutput, calls=%fused_computation.21 | convolution fusion | flops 8589934592 | bytes 27262976 | tf_op jit(solution)/shard_map/dot_general | solution.py:451
  305.6 0.0 copy-done.5
  305.6 52.4 %turn_1.1.refs_5_ = s16[8,2,272,512]{3,2,1,0:T(8,128)(2,1)S(1)} custom-call(f32[512,1024]{1,0:T(8,128)S(1)} %fusion.11.refs_0_.refs_1_), custom_call_target="tpu_custom_call" | custom-call | tf_op jit(solution)/shard_map/turn_1/pallas_call | solution.py:400
  358.0 0.0 copy-start.3
  358.0 2.0 copy-done.3
  360.0 0.0 copy-start.6
  360.0 1.3 copy-done.6
  361.3 80.3 %all-gather.9.cloned.1.call-done = bf16[8192,1024]{1,0:T(8,128)(2,1)} async-done(((bf16[512,1024]{1,0:T(8,128)(2,1)}), bf16[8192,1024]{1,0:T(8,128)(2,1)}) %all-gather.9.cloned.1.call-update) | async-done | bytes 16777232 | tf_op jit(solution)/shard_map/all_gather | solution.py:450
  441.7 14.6 %fusion.12.refs_0_.refs_2_ = f32[512,1024]{1,0:T(8,128)S(1)} fusion(bf16[512,8192]{1,0:T(8,128)(2,1)} %mul.25, bf16[8192,1024]{1,0:T(8,128)(2,1)} %all-gather.9.cloned.1.call-done), kind=kOutput, calls=%fused_computation.22 | convolution fusion | flops 8589934592 | bytes 27262976 | tf_op jit(solution)/shard_map/dot_general | solution.py:451
  456.2 0.0 copy-start.7
  456.3 52.4 %turn_2.1.refs_6_ = s16[8,2,272,512]{3,2,1,0:T(8,128)(2,1)S(1)} custom-call(f32[512,1024]{1,0:T(8,128)S(1)} %fusion.12.refs_0_.refs_2_), custom_call_target="tpu_custom_call" | custom-call | tf_op jit(solution)/shard_map/turn_2/pallas_call | solution.py:400
  508.7 0.0 copy-start.4
  508.7 2.1 copy-done.4
  510.7 81.5 %all-gather.11.cloned.1.call-done = bf16[8192,1024]{1,0:T(8,128)(2,1)} async-done(((bf16[512,1024]{1,0:T(8,128)(2,1)}), bf16[8192,1024]{1,0:T(8,128)(2,1)}) %all-gather.11.cloned.1.call-update) | async-done | bytes 16777232 | tf_op jit(solution)/shard_map/all_gather | solution.py:450
  592.2 15.7 %fusion.13.refs_3_ = f32[512,1024]{1,0:T(8,128)} fusion(bf16[512,8192]{1,0:T(8,128)(2,1)} %mul.25, bf16[8192,1024]{1,0:T(8,128)(2,1)} %all-gather.11.cloned.1.call-done), kind=kOutput, calls=%fused_computation.23 | convolution fusion | flops 8589934592 | bytes 27262976 | tf_op jit(solution)/shard_map/dot_general | solution.py:451
  608.0 0.0 copy-done.7
  608.0 71.8 %turn_3.1 = (f32[512,4096]{1,0:T(8,128)}, f32[3]{0:T(128)}) custom-call(f32[512,1024]{1,0:T(8,128)} %copy-done.5, f32[512,1024]{1,0:T(8,128)} %copy-done.6, f32[512,1024]{1,0:T(8,128)} %copy-done.7, f32[512,1024]{1,0:T(8,128)} %fusion.13.refs_3_, s16[8,2,272,512]{3,2,1,0:T(8,128)(2,1)} %copy-done.2, s16[8,2,272,512]{3,2,1,0:T(8,128)(2,1)} %copy-done.3, ...), custom_call_target="tpu_custom_call" | custom-call | tf_op jit(solution)/shard_map/turn_3/pallas_call | solution.py:400
  679.7 1.3 fusion.9
  682.4 0.0 copy-start.1
  682.4 7.9 %broadcast_multiply_fusion = f32[512,4096]{1,0:T(8,128)} fusion(f32[512,4096]{1,0:T(8,128)} %get-tuple-element.4, f32[]{:T(128)} %bitcast.5), kind=kLoop, calls=%fused_computation | loop fusion | flops 2097152 | bytes 16777220 | tf_op jit(solution)/shard_map/mul | solution.py:456
  690.3 1.2 pad_maximum_fusion.4
  691.5 0.0 copy-done.1
  (4 shorter events, 0.1 us)
Async XLA Ops:
  7.2 72.0 %copy-start = (f32[16,16]{1,0:T(8,128)S(1)}, f32[16,16]{1,0:T(8,128)}, u32[]{:S(2)}) copy-start(f32[16,16]{1,0:T(8,128)} %param.11) | copy-start | bytes 3076
  7.2 133.1 %all-gather.5.cloned.1.call-start = ((), (), s32[]{:S(2)}) async-start(), calls=%async_computation | async-start | bytes 17825792 | tf_op jit(solution)/shard_map/all_gather | solution.py:450
  9.8 5.0 copy-start.9
  11.0 280.0 %all-gather.7.cloned.1.call-start = ((), (), s32[]{:S(2)}) async-start(), calls=%async_computation.1 | async-start | bytes 17825792 | tf_op jit(solution)/shard_map/all_gather | solution.py:450
  12.2 429.4 %all-gather.9.cloned.1.call-start = ((), (), s32[]{:S(2)}) async-start(), calls=%async_computation.2 | async-start | bytes 17825792 | tf_op jit(solution)/shard_map/all_gather | solution.py:450
  13.4 578.8 %all-gather.11.cloned.1.call-start = ((), (), s32[]{:S(2)}) async-start(), calls=%async_computation.3 | async-start | bytes 17825792 | tf_op jit(solution)/shard_map/all_gather | solution.py:450
  26.8 42.1 %copy-start.8 = (s32[16,8192]{1,0:T(8,128)S(1)}, s32[16,8192]{1,0:T(8,128)}, u32[]{:S(2)}) copy-start(s32[16,8192]{1,0:T(8,128)} %param.9) | copy-start | bytes 1572868
  69.0 9.6 %copy-start.10 = (f32[16]{0:T(128)S(1)}, f32[16]{0:T(128)}, u32[]{:S(2)}) copy-start(f32[16]{0:T(128)} %param.10) | copy-start | bytes 196
  154.9 150.7 %copy-start.5 = (f32[512,1024]{1,0:T(8,128)}, f32[512,1024]{1,0:T(8,128)S(1)}, u32[]{:S(2)}) copy-start(f32[512,1024]{1,0:T(8,128)S(1)} %fusion.10.refs_0_) | copy-start | bytes 6291460
  222.0 2.1 copy-start.2
  358.0 2.0 copy-start.3
  360.0 1.3 copy-start.6
  456.2 151.7 %copy-start.7 = (f32[512,1024]{1,0:T(8,128)}, f32[512,1024]{1,0:T(8,128)S(1)}, u32[]{:S(2)}) copy-start(f32[512,1024]{1,0:T(8,128)S(1)} %fusion.12.refs_0_.refs_2_) | copy-start | bytes 6291460
  508.7 2.1 copy-start.4
  682.4 9.1 %copy-start.1 = (f32[16,16]{1,0:T(8,128)S(1)}, f32[16,16]{1,0:T(8,128)}, u32[]{:S(2)}) copy-start(f32[16,16]{1,0:T(8,128)} %param.11) | copy-start | bytes 3076
Sparse Core Ops, SparseCore 0:
  11.1 129.1 all-gather.4
  142.5 148.4 all-gather.6
  293.2 148.4 all-gather.8
  443.7 148.4 all-gather.10

commit v4 on v3

--- a/solution.py
+++ b/solution.py
@@ -17,8 +17,8 @@
     last = chunk == chunks - 1
     if last:
         products, arrived = refs[:chunks], refs[chunks : 2 * chunks - 1]
-        c_ref, left_ref, right_ref, out_ref, stats_ref, recv = refs[2 * chunks - 1 : 2 * chunks + 5]
-        refs = refs[2 * chunks + 5 :]
+        diagonal_ref, c_ref, out_ref, stats_ref, recv = refs[2 * chunks - 1 : 2 * chunks + 4]
+        refs = refs[2 * chunks + 4 :]
         mine, sums, sum_send, sum_recv = refs[-4:]
     else:
         products = refs[:1]
@@ -52,6 +52,9 @@
         loads = [pltpu.make_async_copy(products[0], p_ref, load_sem.at[0])]
     for load in loads:
         load.start()
+    if last:
+        diagonal_load = pltpu.make_async_copy(diagonal_ref, out_ref, self_sem.at[3])
+        diagonal_load.start()
 
     barrier = pltpu.get_barrier_semaphore()
 
@@ -304,6 +307,7 @@
 
     proj, weight = gather_sums(0)
     theta = 2.0 * proj / weight
+    diagonal_load.wait()
 
     piece = min(128, tile)
 
@@ -321,12 +325,9 @@
                 shrink = jnp.exp2(code * (1.0 / 128.0)) * (1.0 / 32767.0)
                 value = recv[s, h, pl.ds(0, half), rows].astype(jnp.int32).astype(jnp.float32)
                 turned = (value * shrink).T
-                diagonal = jnp.dot(
-                    left_ref[rows, :], right_ref[:, cols], precision=HIGH, preferred_element_type=jnp.float32
-                )
                 sigma = p_ref[rows, cols] + turned
                 residual = sigma - theta * c_ref[rows, cols].astype(jnp.float32)
-                update = residual / jnp.maximum(jnp.abs(diagonal - theta), 1.0)
+                update = residual / jnp.maximum(jnp.abs(out_ref[rows, cols] - theta), 1.0)
                 out_ref[rows, cols] = update
                 squares = squares + fold_sum(residual * residual)
                 spread = spread + fold_sum(update * update)
@@ -348,7 +349,7 @@
     settle()
 
 
-def turn(chunk, chunks, products, arrived, coeff, left, right, strings):
+def turn(chunk, chunks, products, arrived, coeff, diagonal, strings):
     tile_rows, tile_cols = coeff.shape
     row_count = lax.axis_size("row")
     col_count = lax.axis_size("col")
@@ -374,11 +375,11 @@
         dma((others * fold,)),
         dma((others * per,)),
         dma((others * fold,)),
-        dma((3,)),
+        dma((4,)),
     ]
     if last:
-        operands = (*products, *arrived, coeff, left, right)
-        in_specs = [anywhere] * (2 * chunks - 1) + [vmem] * 3
+        operands = (*products, *arrived, diagonal, coeff)
+        in_specs = [anywhere] * (2 * chunks) + [vmem]
         out_shape = (
             jax.ShapeDtypeStruct((tile_rows, tile_cols), jnp.float32),
             jax.ShapeDtypeStruct((3,), jnp.float32),
@@ -410,7 +411,7 @@
     )(*operands)
 
 
-CHUNKS = 4
+CHUNKS = 2
 
 
 def body(ham, coeff, tile_mask, occupation, orbital_energy, coulomb):
@@ -428,17 +429,8 @@
     occ_beta = lax.dynamic_slice_in_dim(occ_float, lax.axis_index("col") * tile_cols, tile_cols, 1)
     energy_alpha = jnp.dot(orbital_energy, occ_alpha, precision=HIGH)
     energy_beta = jnp.dot(orbital_energy, occ_beta, precision=HIGH)
-    mixed = jnp.dot(occ_alpha.T, coulomb, precision=HIGH)
-    orbitals = occupation.shape[0]
-    depth = -(-(orbitals + 2) // 128) * 128
-    left = jnp.concatenate(
-        [mixed, energy_alpha[:, None], jnp.ones((tile_rows, 1)), jnp.zeros((tile_rows, depth - orbitals - 2))],
-        axis=1,
-    )
-    right = jnp.concatenate(
-        [occ_beta, jnp.ones((1, tile_cols)), energy_beta[None, :], jnp.zeros((depth - orbitals - 2, tile_cols))],
-        axis=0,
-    )
+    coupling = jnp.dot(jnp.dot(occ_alpha.T, coulomb, precision=HIGH), occ_beta, precision=HIGH)
+    diagonal = energy_alpha[:, None] + energy_beta[None, :] + coupling
     fold = tile_cols // tile_rows
     chunks = math.gcd(CHUNKS, fold)
     products = []
@@ -449,7 +441,7 @@
         )
         gathered = with_layout_constraint(lax.all_gather(part, "row", axis=0, tiled=True), Layout((0, 1)))
         products.append(jnp.dot(masked, gathered, preferred_element_type=jnp.float32))
-        result = turn(q, chunks, products, arrived, coeff, left, right, strings)
+        result = turn(q, chunks, products, arrived, coeff, diagonal, strings)
         if q < chunks - 1:
             arrived.append(result)
     update, sums = result

time: 699 us -> 532 us (0.76)
  waiting for transfers between devices: 287 us -> 191 us
  Pallas kernels: 244 us -> 187 us
  other arithmetic: 25.6 us -> 12.4 us
    all_gather x4 -> x2, waiting for transfers between devices: 286 us -> 191 us  [body(): lax.all_gather(part, 'row', axis=0, tiled=True)]
    pallas_call x4 -> x2, Pallas kernels: 244 us -> 187 us  [turn(): pl.pallas_call(functools.partial(turn_kernel, row_count, col_count, float...]
    mul x1 -> x0, other arithmetic: 9.58 us -> none  [body(): ham.reshape(mask_rows, block_size, mask_cols, block_size) * weights]
    dot_general x1 -> x2, matrix products: 0.6 us -> 9.64 us  [the longest x1 9.04 us: body(): jnp.dot(jnp.dot(occ_alpha.T, coulomb, precision=HIGH), occ_beta, precisio...]
    dot_general x4 -> x2, matrix products: 59.5 us -> 51.9 us  [body(): jnp.dot(masked, gathered, preferred_element_type=jnp.float32)]
  transfers between devices with their start and end apart: 4 -> 2, of which waited for: 4 -> 2; matrix products, arithmetic and copies ran while one was open for 16% -> 17% of each run, Pallas kernels for 25% -> 19%
where the time goes in v4:
time: 532 us; the launch traced here: 530 us
  waiting for transfers between devices  191 us (36%)
  Pallas kernels  187 us (35%)
  local copies, waits for them, and re-layouts  62.5 us (12%)
  matrix products  61.9 us (12%)
  between operations  15.5 us (3%)
  other arithmetic  12.4 us (2%)
    all_gather x2, waiting for transfers between devices, body(): lax.all_gather(part, 'row', axis=0, tiled=True)  191 us
    pallas_call x2, Pallas kernels, turn(): pl.pallas_call(functools.partial(turn_kernel, row_count, col_count, float...  187 us
    mul x2, local copies, waits for them, and re-layouts, body(): ham.reshape(mask_rows, block_size, mask_cols, block_size) * weights  54.4 us
    dot_general x2, matrix products, body(): jnp.dot(masked, gathered, preferred_element_type=jnp.float32)  51.9 us
  transfers between devices with their start and end apart: 2, of which 2 were waited for; matrix products, arithmetic and copies ran while one was open for 17% of the time, Pallas kernels for 19%

profile of v4, /device:TPU:0, one launch (start us, length us, event | category | flops | bytes accessed | tf_op | source)
XLA Modules:
  0.0 530.4 jit_solution(11912031971470785954)
XLA Ops:
  7.2 0.0 copy-start
  7.2 0.0 all-gather.3.cloned.1.call-start
  7.2 2.6 fusion.17
  9.8 0.0 copy-start.5
  9.8 1.6 pad_maximum_fusion
  11.5 0.0 all-gather.3.cloned.1.call-update
  11.5 0.0 all-gather.5.cloned.1.call-start
  11.5 1.6 pad_maximum_fusion.1
  13.2 0.0 all-gather.5.cloned.1.call-update
  13.2 0.0 copy-done.5
  13.2 12.3 %mul.23 = bf16[16,32,256,32]{3,2,1,0:T(8,128)(2,1)} broadcast(bf16[16,256]{1,0:T(8,128)(2,1)S(1)} %convert_element_type.6), dimensions={0,2} | broadcast | bytes 8396800 | tf_op jit(solution)/shard_map/mul | solution.py:424
  25.5 0.0 copy-start.4
  25.5 0.0 copy-start.6
  25.5 42.1 %mul.24 = bf16[512,8192]{1,0:T(8,128)(2,1)} reshape(bf16[16,32,256,32]{3,2,1,0:T(8,128)(2,1)} %mul.23) | data formatting | bytes 16777216 | tf_op jit(solution)/shard_map/mul | solution.py:424
  67.6 0.0 copy-done.4
  67.6 0.0 copy-done.6
  67.6 0.1 fusion.9
  67.8 0.3 fusion.5
  68.1 0.0 copy-done
  68.1 0.6 fusion.7
  68.7 9.0 %add_add_fusion.refs_3_ = f32[512,4096]{1,0:T(8,128)} fusion(f32[512,16]{1,0:T(8,128)S(1)} %fusion.7, f32[4096]{0:T(1024)S(1)} %bitcast.15, f32[512]{0:T(512)S(1)} %bitcast.16, f32[16,8192]{1,0:T(8,128)S(1)} %convert_element_type.7, s32[]{:T(128)S(6)} %select_n.7), kind=kOutput, calls=%fused_computation | convolution fusion | flops 406847488 | bytes 8931332 | tf_op jit(solution)/shard_map/dot_general | solution.py:432
  77.8 104.6 %all-gather.3.cloned.1.call-done = bf16[8192,2048]{1,0:T(8,128)(2,1)} async-done(((bf16[512,2048]{1,0:T(8,128)(2,1)}), bf16[8192,2048]{1,0:T(8,128)(2,1)}) %all-gather.3.cloned.1.call-update) | async-done | bytes 33554448 | tf_op jit(solution)/shard_map/all_gather | solution.py:442
  182.4 24.6 %fusion.2.refs_0_ = f32[512,2048]{1,0:T(8,128)S(1)} fusion(bf16[8192,2048]{1,0:T(8,128)(2,1)} %all-gather.3.cloned.1.call-done, bf16[512,8192]{1,0:T(8,128)(2,1)} %param.6, bf16[512,8192]{1,0:T(8,128)(2,1)} %mul.24), kind=kOutput, calls=%fused_computation.4 | convolution fusion | flops 17184063488 | bytes 54525952 | tf_op jit(solution)/shard_map/dot_general | solution.py:443
  207.1 102.5 %turn_0.1.refs_2_ = s16[8,2,272,512]{3,2,1,0:T(8,128)(2,1)S(1)} custom-call(f32[512,2048]{1,0:T(8,128)S(1)} %fusion.2.refs_0_), custom_call_target="tpu_custom_call" | custom-call | tf_op jit(solution)/shard_map/turn_0/pallas_call | solution.py:401
  309.6 0.0 copy-start.2
  309.6 2.1 copy-done.2
  311.7 0.0 copy-start.3
  311.7 2.0 copy-done.3
  313.7 86.1 %all-gather.5.cloned.1.call-done = bf16[8192,2048]{1,0:T(8,128)(2,1)} async-done(((bf16[512,2048]{1,0:T(8,128)(2,1)}), bf16[8192,2048]{1,0:T(8,128)(2,1)}) %all-gather.5.cloned.1.call-update) | async-done | bytes 33554448 | tf_op jit(solution)/shard_map/all_gather | solution.py:442
  399.8 27.2 %fusion.refs_1_ = f32[512,2048]{1,0:T(8,128)} fusion(bf16[8192,2048]{1,0:T(8,128)(2,1)} %all-gather.5.cloned.1.call-done, bf16[512,8192]{1,0:T(8,128)(2,1)} %param.6, bf16[512,8192]{1,0:T(8,128)(2,1)} %mul.24), kind=kOutput, calls=%fused_computation.2 | convolution fusion | flops 17184063488 | bytes 54525952 | tf_op jit(solution)/shard_map/dot_general | solution.py:443
  427.0 84.7 %turn_1.1 = (f32[512,4096]{1,0:T(8,128)}, f32[3]{0:T(128)}) custom-call(f32[512,2048]{1,0:T(8,128)} %copy-done.3, f32[512,2048]{1,0:T(8,128)} %fusion.refs_1_, s16[8,2,272,512]{3,2,1,0:T(8,128)(2,1)} %copy-done.2, f32[512,4096]{1,0:T(8,128)} %add_add_fusion.refs_3_, bf16[512,4096]{1,0:T(8,128)(2,1)} %refs_4_.1), custom_call_target="tpu_custom_call" | custom-call | tf_op jit(solution)/shard_map/turn_1/pallas_call | solution.py:401
  511.7 1.4 fusion.18
  514.5 0.0 copy-start.1
  514.5 7.9 %broadcast_multiply_fusion = f32[512,4096]{1,0:T(8,128)} fusion(f32[512,4096]{1,0:T(8,128)} %get-tuple-element.4, f32[]{:T(128)} %bitcast.4), kind=kLoop, calls=%fused_computation.1 | loop fusion | flops 2097152 | bytes 16777220 | tf_op jit(solution)/shard_map/mul | solution.py:448
  522.4 1.2 pad_maximum_fusion.2
  523.6 0.0 copy-done.1
  (2 shorter events, 0.0 us)
Async XLA Ops:
  7.2 60.9 %copy-start = (f32[16,16]{1,0:T(8,128)S(1)}, f32[16,16]{1,0:T(8,128)}, u32[]{:S(2)}) copy-start(f32[16,16]{1,0:T(8,128)} %param.11) | copy-start | bytes 3076
  7.2 175.2 %all-gather.3.cloned.1.call-start = ((), (), s32[]{:S(2)}) async-start(), calls=%async_computation | async-start | bytes 35651584 | tf_op jit(solution)/shard_map/all_gather | solution.py:442
  9.8 3.4 copy-start.5
  11.5 388.3 %all-gather.5.cloned.1.call-start = ((), (), s32[]{:S(2)}) async-start(), calls=%async_computation.1 | async-start | bytes 35651584 | tf_op jit(solution)/shard_map/all_gather | solution.py:442
  25.5 42.1 %copy-start.4 = (s32[16,8192]{1,0:T(8,128)S(1)}, s32[16,8192]{1,0:T(8,128)}, u32[]{:S(2)}) copy-start(s32[16,8192]{1,0:T(8,128)} %param.9) | copy-start | bytes 1572868
  25.5 42.2 %copy-start.6 = (f32[16]{0:T(128)S(1)}, f32[16]{0:T(128)}, u32[]{:S(2)}) copy-start(f32[16]{0:T(128)} %param.10) | copy-start | bytes 196
  309.6 2.1 copy-start.2
  311.7 2.0 copy-start.3
  514.5 9.1 %copy-start.1 = (f32[16,16]{1,0:T(8,128)S(1)}, f32[16,16]{1,0:T(8,128)}, u32[]{:S(2)}) copy-start(f32[16,16]{1,0:T(8,128)} %param.11) | copy-start | bytes 3076
Sparse Core Ops, SparseCore 0:
  11.6 170.7 all-gather.2
  184.0 215.7 all-gather.4

commit v5 on v4

--- a/solution.py
+++ b/solution.py
@@ -1,5 +1,4 @@
 import functools
-import math
 
 import jax
 import jax.numpy as jnp
@@ -11,6 +10,11 @@
 
 MESH = pl.DeviceIdType.MESH
 HIGH = lax.Precision.HIGHEST
+STRIDE = 4
+
+
+def members(chunk, chunks, fold):
+    return [s for s in range(fold) if (s % STRIDE == STRIDE - 1) == (chunk == chunks - 1)]
 
 
 def turn_kernel(row_count, col_count, total, chunk, chunks, *refs):
@@ -30,23 +34,25 @@
     tile = p_ref.shape[0]
     half = tile // 2
     fold = row_count // col_count
-    per = fold // chunks
+    per = len(members(chunk, chunks, fold))
     home = lax.div(row, fold)
     place = lax.rem(row, fold)
-    turn = lax.div(place, chunks)
+    turn = lax.div(place, STRIDE)
+    if not last:
+        turn = lax.rem(turn * (STRIDE - 1) + lax.rem(place, STRIDE), per)
     count = row_count * col_count
     me = row * col_count + col
     is_home = home == col
-    takes = lax.rem(place, chunks) == chunk
+    takes = (lax.rem(place, STRIDE) == STRIDE - 1) if last else (lax.rem(place, STRIDE) < STRIDE - 1)
     if last:
         loads = [
             pltpu.make_async_copy(
                 product.at[:, pl.ds(k * tile, tile)],
-                p_ref.at[:, pl.ds((q + chunks * k) * tile, tile)],
-                load_sem.at[q * per + k],
+                p_ref.at[:, pl.ds(s * tile, tile)],
+                load_sem.at[s],
             )
             for q, product in enumerate(products)
-            for k in range(per)
+            for k, s in enumerate(members(q, chunks, fold))
         ]
     else:
         loads = [pltpu.make_async_copy(products[0], p_ref, load_sem.at[0])]
@@ -88,7 +94,9 @@
 
     def spot(k):
         kk = lax.rem(turn + k, per)
-        return kk, chunk + chunks * kk
+        if last:
+            return kk, kk * STRIDE + STRIDE - 1
+        return kk, lax.div(kk, STRIDE - 1) * STRIDE + lax.rem(kk, STRIDE - 1)
 
     def own_direct(k):
         kk, s = spot(k)
@@ -297,9 +305,9 @@
         settle()
         return
 
-    for q, ready in enumerate(arrived):
-
-        @pl.when(lax.rem(place, chunks) == q)
+    for ready in arrived:
+
+        @pl.when(jnp.logical_not(takes))
         def _():
             fetch = pltpu.make_async_copy(ready, recv, self_sem.at[2])
             fetch.start()
@@ -354,7 +362,7 @@
     row_count = lax.axis_size("row")
     col_count = lax.axis_size("col")
     fold = row_count // col_count
-    per = fold // chunks
+    per = len(members(chunk, chunks, fold))
     count = row_count * col_count
     tall = tile_rows // 2 + 16
     others = max(col_count - 1, 1)
@@ -364,7 +372,7 @@
     last = chunk == chunks - 1
     arrival = (fold, 2, tall, tile_rows)
     scratch = [
-        pltpu.VMEM((tile_rows, tile_cols if last else tile_cols // chunks), jnp.float32),
+        pltpu.VMEM((tile_rows, tile_cols if last else per * tile_rows), jnp.float32),
         pltpu.VMEM((per, 2, tall, tile_rows), jnp.int16),
         pltpu.VMEM((others, per, tall, tile_rows), jnp.int16),
         pltpu.VMEM((others * fold, tall, tile_rows), jnp.int16),
@@ -411,9 +419,6 @@
     )(*operands)
 
 
-CHUNKS = 2
-
-
 def body(ham, coeff, tile_mask, occupation, orbital_energy, coulomb):
     tile_rows, strings = ham.shape
     tile_cols = coeff.shape[1]
@@ -432,12 +437,12 @@
     coupling = jnp.dot(jnp.dot(occ_alpha.T, coulomb, precision=HIGH), occ_beta, precision=HIGH)
     diagonal = energy_alpha[:, None] + energy_beta[None, :] + coupling
     fold = tile_cols // tile_rows
-    chunks = math.gcd(CHUNKS, fold)
+    chunks = 2
     products = []
     arrived = []
     for q in range(chunks):
         part = jnp.concatenate(
-            [coeff[:, s * tile_rows : (s + 1) * tile_rows] for s in range(q, fold, chunks)], axis=1
+            [coeff[:, s * tile_rows : (s + 1) * tile_rows] for s in members(q, chunks, fold)], axis=1
         )
         gathered = with_layout_constraint(lax.all_gather(part, "row", axis=0, tiled=True), Layout((0, 1)))
         products.append(jnp.dot(masked, gathered, preferred_element_type=jnp.float32))

time: 532 us -> 612 us (1.15)
  waiting for transfers between devices: 191 us -> 288 us
  Pallas kernels: 187 us -> 169 us
    all_gather x2, waiting for transfers between devices: 191 us -> 288 us  [body(): lax.all_gather(part, 'row', axis=0, tiled=True)]
    pallas_call x2, Pallas kernels: 187 us -> 169 us  [turn(): pl.pallas_call(functools.partial(turn_kernel, row_count, col_count, float...]
  transfers between devices with their start and end apart: 2 -> 2, of which waited for: 2 -> 2; matrix products, arithmetic and copies ran while one was open for 17% -> 14% of each run, Pallas kernels for 19% -> 0%
where the time goes in v5:
time: 612 us; the launch traced here: 611 us
  waiting for transfers between devices  288 us (47%)
  Pallas kernels  169 us (28%)
  local copies, waits for them, and re-layouts  63.5 us (10%)
  matrix products  63 us (10%)
  between operations  15.5 us (3%)
  other arithmetic  12.2 us (2%)
    all_gather x2, waiting for transfers between devices, body(): lax.all_gather(part, 'row', axis=0, tiled=True)  288 us
    pallas_call x2, Pallas kernels, turn(): pl.pallas_call(functools.partial(turn_kernel, row_count, col_count, float...  169 us
    mul x2, local copies, waits for them, and re-layouts, body(): ham.reshape(mask_rows, block_size, mask_cols, block_size) * weights  54 us
    dot_general x2, matrix products, body(): jnp.dot(masked, gathered, preferred_element_type=jnp.float32)  52.9 us
  transfers between devices with their start and end apart: 2, of which 2 were waited for; matrix products, arithmetic and copies ran while one was open for 14% of the time, Pallas kernels for 0%

profile of v5, /device:TPU:0, one launch (start us, length us, event | category | flops | bytes accessed | tf_op | source)
XLA Modules:
  0.0 611.0 jit_solution(17273148390870728319)
XLA Ops:
  7.2 0.0 copy-start
  7.2 0.0 all-gather.5.cloned.1.call-start
  7.2 1.3 fusion.17
  8.5 1.1 pad_maximum_fusion.1
  9.6 0.0 copy-start.5
  9.6 0.0 all-gather.5.cloned.1.call-update
  9.7 0.0 all-gather.3.cloned.1.call-start
  9.7 2.1 fusion.18
  11.8 2.0 pad_maximum_fusion
  13.8 0.0 all-gather.3.cloned.1.call-update
  13.8 0.0 copy-done.5
  13.9 12.0 %mul.23 = bf16[16,32,256,32]{3,2,1,0:T(8,128)(2,1)} broadcast(bf16[16,256]{1,0:T(8,128)(2,1)S(1)} %convert_element_type.6), dimensions={0,2} | broadcast | bytes 8396800 | tf_op jit(solution)/shard_map/mul | solution.py:429
  25.8 0.0 copy-start.4
  25.8 0.0 copy-start.6
  25.8 42.1 %mul.24 = bf16[512,8192]{1,0:T(8,128)(2,1)} reshape(bf16[16,32,256,32]{3,2,1,0:T(8,128)(2,1)} %mul.23) | data formatting | bytes 16777216 | tf_op jit(solution)/shard_map/mul | solution.py:429
  67.9 0.0 copy-done.4
  67.9 0.0 copy-done.6
  67.9 0.1 fusion.9
  68.1 0.3 fusion.5
  68.4 0.0 copy-done
  68.4 0.6 fusion.7
  69.0 9.1 %add_add_fusion.refs_3_ = f32[512,4096]{1,0:T(8,128)} fusion(f32[512,16]{1,0:T(8,128)S(1)} %fusion.7, f32[4096]{0:T(1024)S(1)} %bitcast.15, f32[512]{0:T(512)S(1)} %bitcast.16, f32[16,8192]{1,0:T(8,128)S(1)} %convert_element_type.7, s32[]{:T(128)S(6)} %select_n.7), kind=kOutput, calls=%fused_computation | convolution fusion | flops 406847488 | bytes 8931332 | tf_op jit(solution)/shard_map/dot_general | solution.py:437
  78.1 61.3 %all-gather.5.cloned.1.call-done = bf16[8192,1024]{1,0:T(8,128)(2,1)} async-done(((bf16[512,1024]{1,0:T(8,128)(2,1)}), bf16[8192,1024]{1,0:T(8,128)(2,1)}) %all-gather.5.cloned.1.call-update) | async-done | bytes 16777232 | tf_op jit(solution)/shard_map/all_gather | solution.py:447
  139.4 20.0 %fusion.refs_1_ = f32[512,1024]{1,0:T(8,128)} fusion(bf16[8192,1024]{1,0:T(8,128)(2,1)} %all-gather.5.cloned.1.call-done, bf16[512,8192]{1,0:T(8,128)(2,1)} %param.6, bf16[512,8192]{1,0:T(8,128)(2,1)} %mul.24), kind=kOutput, calls=%fused_computation.2 | convolution fusion | flops 8594128896 | bytes 35651584 | tf_op jit(solution)/shard_map/dot_general | solution.py:448
  159.4 226.8 %all-gather.3.cloned.1.call-done = bf16[8192,3072]{1,0:T(8,128)(2,1)} async-done(((bf16[512,3072]{1,0:T(8,128)(2,1)}), bf16[8192,3072]{1,0:T(8,128)(2,1)}) %all-gather.3.cloned.1.call-update) | async-done | bytes 50331664 | tf_op jit(solution)/shard_map/all_gather | solution.py:447
  386.2 32.8 %fusion.2.refs_0_ = f32[512,3072]{1,0:T(8,128)S(1)} fusion(bf16[8192,3072]{1,0:T(8,128)(2,1)} %all-gather.3.cloned.1.call-done, bf16[512,8192]{1,0:T(8,128)(2,1)} %param.6, bf16[512,8192]{1,0:T(8,128)(2,1)} %mul.24), kind=kOutput, calls=%fused_computation.4 | convolution fusion | flops 25773998080 | bytes 73400320 | tf_op jit(solution)/shard_map/dot_general | solution.py:448
  419.1 96.8 %turn_0.1.refs_2_ = s16[8,2,272,512]{3,2,1,0:T(8,128)(2,1)S(1)} custom-call(f32[512,3072]{1,0:T(8,128)S(1)} %fusion.2.refs_0_), custom_call_target="tpu_custom_call" | custom-call | tf_op jit(solution)/shard_map/turn_0/pallas_call | solution.py:409
  515.9 0.0 copy-start.2
  515.9 2.7 copy-done.2
  518.6 0.0 copy-start.3
  518.6 2.1 copy-done.3
  520.7 71.8 %turn_1.1 = (f32[512,4096]{1,0:T(8,128)}, f32[3]{0:T(128)}) custom-call(f32[512,3072]{1,0:T(8,128)} %copy-done.2, f32[512,1024]{1,0:T(8,128)} %fusion.refs_1_, s16[8,2,272,512]{3,2,1,0:T(8,128)(2,1)} %copy-done.3, f32[512,4096]{1,0:T(8,128)} %add_add_fusion.refs_3_, bf16[512,4096]{1,0:T(8,128)(2,1)} %refs_4_.1), custom_call_target="tpu_custom_call" | custom-call | tf_op jit(solution)/shard_map/turn_1/pallas_call | solution.py:409
  592.5 1.3 fusion.19
  595.2 0.0 copy-start.1
  595.2 7.9 %broadcast_multiply_fusion = f32[512,4096]{1,0:T(8,128)} fusion(f32[512,4096]{1,0:T(8,128)} %get-tuple-element.4, f32[]{:T(128)} %bitcast.4), kind=kLoop, calls=%fused_computation.1 | loop fusion | flops 2097152 | bytes 16777220 | tf_op jit(solution)/shard_map/mul | solution.py:453
  603.0 1.1 pad_maximum_fusion.2
  604.2 0.0 copy-done.1
  (2 shorter events, 0.0 us)
Async XLA Ops:
  7.2 61.2 %copy-start = (f32[16,16]{1,0:T(8,128)S(1)}, f32[16,16]{1,0:T(8,128)}, u32[]{:S(2)}) copy-start(f32[16,16]{1,0:T(8,128)} %param.11) | copy-start | bytes 3076
  7.2 132.2 %all-gather.5.cloned.1.call-start = ((), (), s32[]{:S(2)}) async-start(), calls=%async_computation.1 | async-start | bytes 17825792 | tf_op jit(solution)/shard_map/all_gather | solution.py:447
  9.6 4.2 copy-start.5
  9.7 376.6 %all-gather.3.cloned.1.call-start = ((), (), s32[]{:S(2)}) async-start(), calls=%async_computation | async-start | bytes 53477376 | tf_op jit(solution)/shard_map/all_gather | solution.py:447
  25.8 42.1 %copy-start.4 = (s32[16,8192]{1,0:T(8,128)S(1)}, s32[16,8192]{1,0:T(8,128)}, u32[]{:S(2)}) copy-start(s32[16,8192]{1,0:T(8,128)} %param.9) | copy-start | bytes 1572868
  25.8 42.1 %copy-start.6 = (f32[16]{0:T(128)S(1)}, f32[16]{0:T(128)}, u32[]{:S(2)}) copy-start(f32[16]{0:T(128)} %param.10) | copy-start | bytes 196
  515.9 2.7 copy-start.2
  518.6 2.1 copy-start.3
  595.2 9.0 %copy-start.1 = (f32[16,16]{1,0:T(8,128)S(1)}, f32[16,16]{1,0:T(8,128)}, u32[]{:S(2)}) copy-start(f32[16,16]{1,0:T(8,128)} %param.11) | copy-start | bytes 3076
Sparse Core Ops, SparseCore 0:
  10.1 129.1 all-gather.4
  141.0 245.2 all-gather.2

commit v6 on v5

--- a/solution.py
+++ b/solution.py
@@ -444,6 +444,8 @@
         part = jnp.concatenate(
             [coeff[:, s * tile_rows : (s + 1) * tile_rows] for s in members(q, chunks, fold)], axis=1
         )
+        if q > 0:
+            part, gathered = lax.optimization_barrier((part, gathered))
         gathered = with_layout_constraint(lax.all_gather(part, "row", axis=0, tiled=True), Layout((0, 1)))
         products.append(jnp.dot(masked, gathered, preferred_element_type=jnp.float32))
         result = turn(q, chunks, products, arrived, coeff, diagonal, strings)

time: 612 us -> 588 us (0.961)
  waiting for transfers between devices: 288 us -> 248 us
  Pallas kernels: 169 us -> 186 us
    all_gather x2, waiting for transfers between devices: 288 us -> 247 us  [body(): lax.all_gather(part, 'row', axis=0, tiled=True)]
    pallas_call x2, Pallas kernels: 169 us -> 186 us  [turn(): pl.pallas_call(functools.partial(turn_kernel, row_count, col_count, float...]
  transfers between devices with their start and end apart: 2 -> 2, of which waited for: 2 -> 1; matrix products, arithmetic and copies ran while one was open for 14% -> 17% of each run, Pallas kernels for 0% -> 19%
where the time goes in v6:
time: 588 us; the launch traced here: 586 us
  waiting for transfers between devices  248 us (42%)
  Pallas kernels  186 us (32%)
  local copies, waits for them, and re-layouts  63.1 us (11%)
  matrix products  61.3 us (10%)
  between operations  15.5 us (3%)
  other arithmetic  12.3 us (2%)
    all_gather x2, waiting for transfers between devices, body(): lax.all_gather(part, 'row', axis=0, tiled=True)  247 us
    pallas_call x2, Pallas kernels, turn(): pl.pallas_call(functools.partial(turn_kernel, row_count, col_count, float...  186 us
    mul x2, local copies, waits for them, and re-layouts, body(): ham.reshape(mask_rows, block_size, mask_cols, block_size) * weights  53.7 us
    dot_general x2, matrix products, body(): jnp.dot(masked, gathered, preferred_element_type=jnp.float32)  51.2 us
  transfers between devices with their start and end apart: 2, of which 1 were waited for; matrix products, arithmetic and copies ran while one was open for 17% of the time, Pallas kernels for 19%

profile of v6, /device:TPU:0, one launch (start us, length us, event | category | flops | bytes accessed | tf_op | source)
XLA Modules:
  0.0 586.3 jit_solution(13891534610345151569)
XLA Ops:
  7.2 0.0 copy-start
  7.2 0.0 all-gather.3.cloned.1.call-start
  7.2 2.1 fusion.18
  9.3 0.0 copy-start.5
  9.3 2.0 pad_maximum_fusion
  11.4 0.0 all-gather.3.cloned.1.call-update
  11.4 0.0 all-gather.5.cloned.1.call-start
  11.5 1.3 fusion.17
  12.7 1.1 pad_maximum_fusion.1
  13.8 247.5 %all-gather.3.cloned.1.call-done = bf16[8192,3072]{1,0:T(8,128)(2,1)} async-done(((bf16[512,3072]{1,0:T(8,128)(2,1)}), bf16[8192,3072]{1,0:T(8,128)(2,1)}) %all-gather.3.cloned.1.call-update) | async-done | bytes 50331664 | tf_op jit(solution)/shard_map/all_gather | solution.py:449
  261.3 0.0 all-gather.5.cloned.1.call-update
  261.4 0.0 copy-done.5
  261.4 11.9 %mul.23 = bf16[16,32,256,32]{3,2,1,0:T(8,128)(2,1)} broadcast(bf16[16,256]{1,0:T(8,128)(2,1)S(1)} %convert_element_type.6), dimensions={0,2} | broadcast | bytes 8396800 | tf_op jit(solution)/shard_map/mul | solution.py:429
  273.3 0.0 copy-start.4
  273.3 0.0 copy-start.6
  273.3 41.7 %mul.24 = bf16[512,8192]{1,0:T(8,128)(2,1)} reshape(bf16[16,32,256,32]{3,2,1,0:T(8,128)(2,1)} %mul.23) | data formatting | bytes 16777216 | tf_op jit(solution)/shard_map/mul | solution.py:429
  315.1 0.0 copy-done.4
  315.1 0.0 copy-done.6
  315.1 0.1 fusion.9
  315.3 0.3 fusion.5
  315.6 0.0 copy-done
  315.6 0.6 fusion.7
  316.2 9.1 %add_add_fusion.refs_3_ = f32[512,4096]{1,0:T(8,128)} fusion(f32[512,16]{1,0:T(8,128)S(1)} %fusion.7, f32[4096]{0:T(1024)S(1)} %bitcast.15, f32[512]{0:T(512)S(1)} %bitcast.16, f32[16,8192]{1,0:T(8,128)S(1)} %convert_element_type.7, s32[]{:T(128)S(6)} %select_n.7), kind=kOutput, calls=%fused_computation | convolution fusion | flops 406847488 | bytes 8931332 | tf_op jit(solution)/shard_map/dot_general | solution.py:437
  325.2 33.0 %fusion.2.refs_0_ = f32[512,3072]{1,0:T(8,128)S(1)} fusion(bf16[8192,3072]{1,0:T(8,128)(2,1)} %all-gather.3.cloned.1.call-done, bf16[512,8192]{1,0:T(8,128)(2,1)} %param.6, bf16[512,8192]{1,0:T(8,128)(2,1)} %mul.24), kind=kOutput, calls=%fused_computation.4 | convolution fusion | flops 25773998080 | bytes 73400320 | tf_op jit(solution)/shard_map/dot_general | solution.py:450
  358.2 109.8 %turn_0.1.refs_2_ = s16[8,2,272,512]{3,2,1,0:T(8,128)(2,1)S(1)} custom-call(f32[512,3072]{1,0:T(8,128)S(1)} %fusion.2.refs_0_), custom_call_target="tpu_custom_call" | custom-call | tf_op jit(solution)/shard_map/turn_0/pallas_call | solution.py:409
  468.0 0.0 copy-start.2
  468.0 2.7 copy-done.2
  470.7 0.0 copy-start.3
  470.7 2.1 copy-done.3
  472.8 0.0 all-gather.5.cloned.1.call-done
  472.8 18.2 %fusion.refs_1_ = f32[512,1024]{1,0:T(8,128)} fusion(bf16[8192,1024]{1,0:T(8,128)(2,1)} %all-gather.5.cloned.1.call-done, bf16[512,8192]{1,0:T(8,128)(2,1)} %param.6, bf16[512,8192]{1,0:T(8,128)(2,1)} %mul.24), kind=kOutput, calls=%fused_computation.2 | convolution fusion | flops 8594128896 | bytes 35651584 | tf_op jit(solution)/shard_map/dot_general | solution.py:450
  491.0 76.7 %turn_1.1 = (f32[512,4096]{1,0:T(8,128)}, f32[3]{0:T(128)}) custom-call(f32[512,3072]{1,0:T(8,128)} %copy-done.2, f32[512,1024]{1,0:T(8,128)} %fusion.refs_1_, s16[8,2,272,512]{3,2,1,0:T(8,128)(2,1)} %copy-done.3, f32[512,4096]{1,0:T(8,128)} %add_add_fusion.refs_3_, bf16[512,4096]{1,0:T(8,128)(2,1)} %refs_4_.1), custom_call_target="tpu_custom_call" | custom-call | tf_op jit(solution)/shard_map/turn_1/pallas_call | solution.py:409
  567.8 1.3 fusion.19
  570.4 0.0 copy-start.1
  570.4 7.9 %broadcast_multiply_fusion = f32[512,4096]{1,0:T(8,128)} fusion(f32[512,4096]{1,0:T(8,128)} %get-tuple-element.6, f32[]{:T(128)} %bitcast.4), kind=kLoop, calls=%fused_computation.1 | loop fusion | flops 2097152 | bytes 16777220 | tf_op jit(solution)/shard_map/mul | solution.py:455
  578.3 1.2 pad_maximum_fusion.2
  579.5 0.0 copy-done.1
  (2 shorter events, 0.0 us)
Async XLA Ops:
  7.2 308.4 %copy-start = (f32[16,16]{1,0:T(8,128)S(1)}, f32[16,16]{1,0:T(8,128)}, u32[]{:S(2)}) copy-start(f32[16,16]{1,0:T(8,128)} %param.11) | copy-start | bytes 3076
  7.2 254.2 %all-gather.3.cloned.1.call-start = ((), (), s32[]{:S(2)}) async-start(), calls=%async_computation | async-start | bytes 53477376 | tf_op jit(solution)/shard_map/all_gather | solution.py:449
  9.3 252.1 %copy-start.5 = (s32[16,256]{1,0:T(8,128)S(1)}, s32[16,256]{1,0:T(8,128)}, u32[]{:S(2)}) copy-start(s32[16,256]{1,0:T(8,128)} %param.8) | copy-start | bytes 49156
  11.4 461.4 %all-gather.5.cloned.1.call-start = ((), (), s32[]{:S(2)}) async-start(), calls=%async_computation.1 | async-start | bytes 17825792 | tf_op jit(solution)/shard_map/all_gather | solution.py:449
  273.3 41.7 %copy-start.4 = (s32[16,8192]{1,0:T(8,128)S(1)}, s32[16,8192]{1,0:T(8,128)}, u32[]{:S(2)}) copy-start(s32[16,8192]{1,0:T(8,128)} %param.9) | copy-start | bytes 1572868
  273.3 41.8 %copy-start.6 = (f32[16]{0:T(128)S(1)}, f32[16]{0:T(128)}, u32[]{:S(2)}) copy-start(f32[16]{0:T(128)} %param.10) | copy-start | bytes 196
  468.0 2.7 copy-start.2
  470.7 2.1 copy-start.3
  570.4 9.1 %copy-start.1 = (f32[16,16]{1,0:T(8,128)S(1)}, f32[16,16]{1,0:T(8,128)}, u32[]{:S(2)}) copy-start(f32[16,16]{1,0:T(8,128)} %param.11) | copy-start | bytes 3076
Sparse Core Ops, SparseCore 0:
  11.5 249.7 all-gather.2
  263.5 173.3 all-gather.4
